TPU v7x, 32 devices: a whole 2x2x4 slice. The times are simulated.
32 devices in a mesh: dp: 8 (over z, y), mp: 4 (over x, core).
Axes of the slice: x: 2, y: 2, z: 4, core: 2. Of those that a mesh axis runs over, the one named last changes fastest.
Arguments:
- embedded: bfloat16 [32, 64, 4096], P('dp', None, 'mp'), may hold values from -6 to 6
- targets: int32 [32, 64], P('dp'), may hold values from 0 to 65535
- labels: int32 [32], P('dp'), may hold values from 0 to 21
- counts: int32 [8], replicated, may hold values from 0 to 4, as said below
- destinations: int32 [32], P('dp'), may hold values from 0 to 15, as said below
- gain_in: float32 [4096], replicated, may hold values from 0.1 to 1.9
- w_query: bfloat16 [4096, 2048], P(None, 'mp'), may hold values from -40 to 40
- w_key: bfloat16 [4096, 1024], P(None, 'mp'), may hold values from -0.09375 to 0.09375
- w_value: bfloat16 [4096, 1024], P(None, 'mp'), may hold values from -0.09375 to 0.09375
- w_out: bfloat16 [2048, 4096], P('mp'), may hold values from -0.5 to 0.5
- gain_out: float32 [4096], replicated, may hold values from 0.1 to 1.9
- w_vocab: bfloat16 [4096, 65536], P('mp', 'dp'), may hold values from -40 to 40
- prev_probs: float32 [22], replicated, may hold values from 0.03 to 0.2
- log_weights: float32 [22], replicated, may hold values from -200 to 21000
Outputs:
- token_loss: float32 [1024], P(('dp', 'mp'))
- new_weights: float32 [22], replicated
- probs: float32 [22], replicated
Inputs may be any that keep to these rules, and one draw needn't show every extreme that they name: The counts sum to 16. `destinations`: each value from 0 to 15 is held by exactly one live slot; entries of slots that are not live are meaningless.
All inputs are finite; a program needn't handle non-finite values.
Results may differ from a plain program's by a relative error of at most 0.015.
The roundings to bfloat16 on the way count: a program that leaves them out, or rounds other values in their place, can miss the bound.
Values may be sent and summed in bfloat16 or wider, within the bound.
A program may use at most 192 MiB of HBM per device.

v0:
```python
import jax
import jax.numpy as jnp
from jax import lax
from jax.sharding import PartitionSpec as P

HEAD_DIM = 128
DOMAINS = 22
SEQ_DEV = 2


norm_eps = 1e-05
rope_base = 500000.0
memory_rate = 0.9
step_rate = 0.02
explore_mass = 0.005


def normalize(values, gain_vec):
    inv_rms = lax.rsqrt(jnp.mean(values * values, axis=-1, keepdims=True) + norm_eps)
    return values * inv_rms * gain_vec


def rotate_halves(tensor):
    full_width = tensor.shape[-1]
    half_width = full_width // 2
    frequency = jnp.power(
        jnp.float32(rope_base), -jnp.arange(half_width, dtype=jnp.float32) * 2.0 / full_width
    )
    angles = jnp.arange(tensor.shape[1], dtype=jnp.float32)[:, None] * frequency[None, :]
    cosine = jnp.cos(angles)[None, :, None, :]
    sine_part = jnp.sin(angles)[None, :, None, :]
    first_half = tensor[..., :half_width]
    second = tensor[..., half_width:]
    return jnp.concatenate(
        [first_half * cosine - second * sine_part, second * cosine + first_half * sine_part],
        axis=-1,
    )


def local(
    embedded,
    targets,
    labels,
    counts,
    destinations,
    gain_in,
    w_query,
    w_key,
    w_value,
    w_out,
    gain_out,
    w_vocab,
    prev_probs,
    log_weights,
):
    data_count = lax.axis_size("dp")
    data_index = lax.axis_index("dp")
    model_shard_count = lax.axis_size("mp")
    model_index = lax.axis_index("mp")
    slot_count = embedded.shape[0]
    seq_len = embedded.shape[1]
    seq_held = SEQ_DEV
    gathered_rows = (
        lax.all_gather(embedded, "dp", axis=0, tiled=True),
        lax.all_gather(targets, "dp", axis=0, tiled=True),
        lax.all_gather(labels, "dp", axis=0, tiled=True),
        lax.all_gather(destinations, "dp", axis=0, tiled=True),
    )
    slot_ids = jnp.arange(data_count * slot_count, dtype=jnp.int32)
    is_live = slot_ids % slot_count < counts[slot_ids // slot_count]
    wanted = data_index * seq_held + jnp.arange(seq_held, dtype=jnp.int32)
    picking_mask = (gathered_rows[3][None, :] == wanted[:, None]) & is_live[None, :]
    sequence_rows = jnp.einsum(
        "av,vyr->ayr",
        picking_mask.astype(jnp.bfloat16),
        gathered_rows[0],
        preferred_element_type=jnp.float32,
    ).astype(jnp.bfloat16)
    seq_targets = jnp.einsum("gs,sl->gl", picking_mask.astype(jnp.int32), gathered_rows[1])
    seq_labels = jnp.sum(jnp.where(picking_mask, gathered_rows[2][None, :], 0), axis=1).astype(
        jnp.int32
    )
    full_rows = lax.all_gather(sequence_rows, "mp", axis=2, tiled=True)
    rows_all = seq_held * seq_len
    flat_rows = full_rows.reshape(rows_all, -1).astype(jnp.float32)
    normed = normalize(flat_rows, gain_in).astype(jnp.bfloat16)
    local_heads = w_query.shape[1] // HEAD_DIM
    local_groups = w_key.shape[1] // HEAD_DIM
    query_heads = jnp.dot(normed, w_query, preferred_element_type=jnp.float32).reshape(
        seq_held, seq_len, local_heads, HEAD_DIM
    )
    key_heads = jnp.dot(normed, w_key, preferred_element_type=jnp.float32).reshape(
        seq_held, seq_len, local_groups, HEAD_DIM
    )
    value_heads = (
        jnp.dot(normed, w_value, preferred_element_type=jnp.float32)
        .astype(jnp.bfloat16)
        .reshape(seq_held, seq_len, local_groups, HEAD_DIM)
    )
    query_heads = rotate_halves(query_heads).astype(jnp.bfloat16)
    key_heads = rotate_halves(key_heads).astype(jnp.bfloat16)
    group_size = local_heads // local_groups
    key_heads = jnp.repeat(key_heads, group_size, axis=2)
    value_heads = jnp.repeat(value_heads, group_size, axis=2)
    scores = jnp.einsum(
        "sqhe,skhe->shqk", query_heads, key_heads, preferred_element_type=jnp.float32
    ) * HEAD_DIM ** (-0.5)
    causal = jnp.arange(seq_len)[:, None] >= jnp.arange(seq_len)[None, :]
    scores = jnp.where(causal[None, None], scores, -jnp.inf)
    weights = jax.nn.softmax(scores, axis=-1).astype(jnp.bfloat16)
    mixed_heads = jnp.einsum(
        "shqk,skhe->sqhe", weights, value_heads, preferred_element_type=jnp.float32
    )
    mixed_heads = mixed_heads.astype(jnp.bfloat16).reshape(rows_all, local_heads * HEAD_DIM)
    row_block_tiles = rows_all // model_shard_count
    update = lax.psum_scatter(
        jnp.dot(mixed_heads, w_out, preferred_element_type=jnp.float32).astype(jnp.bfloat16),
        "mp",
        scatter_dimension=0,
        tiled=True,
    ).astype(jnp.float32)
    my_start = model_index * row_block_tiles
    own_rows = lax.dynamic_slice_in_dim(flat_rows, my_start, row_block_tiles, 0)
    hidden = own_rows + update
    final_rows = normalize(hidden, gain_out).astype(jnp.bfloat16)
    own_targets = lax.dynamic_slice_in_dim(
        seq_targets.reshape(rows_all), my_start, row_block_tiles, 0
    )
    own_labels = lax.dynamic_slice_in_dim(
        jnp.repeat(seq_labels, seq_len), my_start, row_block_tiles, 0
    )
    everyone = (
        lax.all_gather(final_rows, "dp", axis=0, tiled=True),
        lax.all_gather(own_targets, "dp", axis=0, tiled=True),
        lax.all_gather(own_labels, "dp", axis=0, tiled=True),
    )
    all_rows = everyone[0]
    all_goals = everyone[1]
    all_kinds = everyone[2]
    vocab_local = w_vocab.shape[1]
    logits = jnp.dot(
        all_rows,
        lax.all_gather(w_vocab, "mp", axis=0, tiled=True),
        preferred_element_type=jnp.float32,
    )
    row_top = jnp.max(logits, axis=1)
    spread = jnp.sum(jnp.exp(logits - row_top[:, None]), axis=1)
    column_ids = all_goals - data_index * vocab_local
    picked = jnp.sum(
        jnp.where(
            jnp.arange(vocab_local, dtype=jnp.int32)[None, :] == column_ids[:, None], logits, 0.0
        ),
        axis=1,
    )
    top_all = lax.pmax(row_top, "dp")
    summed = lax.psum((spread * jnp.exp(row_top - top_all), picked), "dp")
    spread_all = summed[0]
    picked_all = summed[1]
    losses = top_all + jnp.log(spread_all) - picked_all
    own_loss = lax.dynamic_slice_in_dim(losses, data_index * row_block_tiles, row_block_tiles, 0)
    domains = jnp.arange(DOMAINS, dtype=jnp.int32)
    member = (all_kinds[:, None] == domains[None, :]).astype(jnp.float32)
    totals = lax.psum((jnp.sum(member * losses[:, None], axis=0), jnp.sum(member, axis=0)), "mp")
    loss_sums = totals[0]
    token_tally = totals[1]
    reward = loss_sums / jnp.maximum(token_tally, 1.0) / prev_probs
    new_weights = memory_rate * log_weights + (1.0 - memory_rate) * reward
    probs = (1.0 - DOMAINS * explore_mass) * jax.nn.softmax(step_rate * new_weights) + explore_mass
    return (own_loss, new_weights, probs)


def solution(mesh):
    placed = (
        P("dp", None, "mp"),
        P("dp", None),
        P("dp"),
        P(),
        P("dp"),
        P(),
        P(None, "mp"),
        P(None, "mp"),
        P(None, "mp"),
        P("mp", None),
        P(),
        P("mp", "dp"),
        P(),
        P(),
    )
    return jax.shard_map(
        local, mesh=mesh, in_specs=placed, out_specs=(P(("dp", "mp")), P(), P()), check_vma=False
    )
```

profile of v0, /device:TPU:0, one launch (start us, length us, event | category | flops | bytes accessed | tf_op | source)
XLA Modules:
  0.0 688.2 jit_solution(7423845925654693603)
XLA Ops:
  8.0 1.2 dynamic-slice
  9.9 0.9 dynamic-update-slice
  10.7 0.8 dynamic-update-slice.2
  11.6 1.4 gather_fusion
  13.0 13.6 %all-reduce.5 = (s32[32]{0:T(128)S(1)}, s32[32]{0:T(128)S(1)}) all-reduce(s32[32]{0:T(128)S(1)} %dynamic-update-slice, s32[32]{0:T(128)S(1)} %dynamic-update-slice.2), channel_id=1, replica_groups=mesh['dp'=8,'mp'=4] {'dp'}, use_global_device_ids=true, to_apply=%add | all-reduce | flops 64 | bytes 512
  27.2 58.5 %all-gather.6.cloned.1.call-done = bf16[32,64,1024]{2,1,0:T(8,128)(2,1)} async-done(((bf16[4,64,1024]{2,1,0:T(8,128)(2,1)}), bf16[32,64,1024]{2,1,0:T(8,128)(2,1)}) %all-gather.6.cloned.1.call-update) | async-done | bytes 4194320 | tf_op jit(solution)/shard_map/all_gather | solution.py:64
  85.7 6.8 fusion.1
  93.3 4.1 copy.67
  97.5 6.5 copy.66
  104.1 4.5 all-gather.8.cloned.1.call-done
  108.7 1.5 multiply_reduce_fusion
  110.3 2.8 fusion.10
  113.2 3.7 fusion.12
  117.2 0.9 fusion.34
  118.2 1.0 fusion.4
  119.5 1.3 copy-done.1
  121.5 1.3 fusion.6
  122.9 3.9 convolution_convert_fusion
  126.9 24.9 %reduce-scatter.2.cloned.1.call-done = bf16[32,4096]{1,0:T(8,128)(2,1)} async-done(((bf16[128,4096]{1,0:T(8,128)(2,1)}), bf16[32,4096]{1,0:T(8,128)(2,1)}) %reduce-scatter.2.cloned.1.call-update) | async-done | bytes 262160 | tf_op jit(solution)/shard_map/reduce_scatter | solution.py:116
  151.8 1.3 multiply_reduce_fusion.1
  153.1 1.9 multiply_convert_fusion.3
  156.5 26.2 %all-gather = s32[8,4,64]{2,1,0:T(4,128)S(1)} all-gather(s32[1,4,64]{2,1,0:T(4,128)S(1)} %bitcast.56), channel_id=1, replica_groups=mesh['dp'=8,'mp'=4] {'dp'}, dimensions={0}, use_global_device_ids=true | all-gather | bytes 9216 | tf_op jit(solution)/shard_map/all_gather | solution.py:65
  183.2 10.0 %all-reduce.4 = (s32[256]{0:T(256)S(1)}, s32[256]{0:T(256)S(1)}) all-reduce(s32[256]{0:T(256)S(1)} %dynamic-slice_dynamic-update-slice_fusion.1, s32[256]{0:T(256)S(1)} %dynamic-slice_dynamic-update-slice_fusion), channel_id=1, replica_groups=mesh['dp'=8,'mp'=4] {'dp'}, use_global_device_ids=true, to_apply=%add.1 | all-reduce | flops 512 | bytes 4096
  193.3 11.1 %all-gather.10.cloned.1.call-done = bf16[256,4096]{1,0:T(8,128)(2,1)} async-done(((bf16[32,4096]{1,0:T(8,128)(2,1)}), bf16[256,4096]{1,0:T(8,128)(2,1)}) %all-gather.10.cloned.1.call-update) | async-done | bytes 2097168 | tf_op jit(solution)/shard_map/all_gather | solution.py:133
  204.4 392.7 %all-gather.12.cloned.1.call-done = bf16[4096,8192]{1,0:T(8,128)(2,1)} async-done(((bf16[1024,8192]{1,0:T(8,128)(2,1)}), bf16[4096,8192]{1,0:T(8,128)(2,1)}) %all-gather.12.cloned.1.call-update) | async-done | bytes 67108880 | tf_op jit(solution)/shard_map/all_gather | solution.py:143
  597.1 30.6 %fusion.37 = (f32[256]{0:T(256)S(1)}, f32[256,8192]{1,0:T(8,128)}) fusion(bf16[256,4096]{1,0:T(8,128)(2,1)} %all-gather.10.cloned.1.call-done, bf16[4096,8192]{1,0:T(8,128)(2,1)} %all-gather.12.cloned.1.call-done), kind=kOutput, calls=%fused_computation.79 | convolution fusion | flops 17181966336 | bytes 77595648 | tf_op jit(solution)/shard_map/dot_general | solution.py:141
  627.7 21.3 %pmax.7 = f32[256]{0:T(256)S(1)} all-reduce(f32[256]{0:T(256)S(1)} %get-tuple-element.25), channel_id=1, replica_groups=mesh['dp'=8,'mp'=4] {'dp'}, use_global_device_ids=true, to_apply=%region_6.7 | all-reduce | flops 256 | bytes 2048 | tf_op jit(solution)/shard_map/pmax | solution.py:155
  649.0 5.1 exponential_reduce_fusion
  654.1 17.1 %all-reduce.6 = (f32[256]{0:T(256)S(1)}, f32[256]{0:T(256)S(1)}) all-reduce(f32[256]{0:T(256)S(1)} %get-tuple-element.4, f32[256]{0:T(256)S(1)} %exponential_multiply_fusion), channel_id=1, replica_groups=mesh['dp'=8,'mp'=4] {'dp'}, use_global_device_ids=true, to_apply=%region_10.11 | all-reduce | flops 512 | bytes 4096 | tf_op jit(solution)/shard_map/psum | solution.py:156
  672.0 6.0 all-reduce.7
  678.6 1.3 fusion.33
  679.9 1.8 multiply_add_fusion
  (71 shorter events, 6.8 us)
Async XLA Ops:
  7.2 113.6 %copy-start = (bf16[4096,256]{1,0:T(8,128)(2,1)S(1)}, bf16[4096,256]{1,0:T(8,128)(2,1)}, u32[]{:S(2)}) copy-start(bf16[4096,256]{1,0:T(8,128)(2,1)} %param.22) | copy-start | bytes 6291460
  7.2 78.5 %all-gather.6.cloned.1.call-start = ((), (), s32[]{:S(2)}) async-start(), calls=%async_computation.1 | async-start | bytes 4718592 | tf_op jit(solution)/shard_map/all_gather | solution.py:64
  7.9 100.7 %all-gather.8.cloned.1.call-start = ((), (), s32[]{:S(2)}) async-start(), calls=%async_computation.2 | async-start | bytes 1310720 | tf_op jit(solution)/shard_map/all_gather | solution.py:83
  93.3 58.5 %reduce-scatter.2.cloned.1.call-start = ((), (), s32[]{:S(2)}) async-start(), calls=%async_computation.3 | async-start | bytes 1310720 | tf_op jit(solution)/shard_map/reduce_scatter | solution.py:116
  97.5 12.8 %copy-start.3 = (f32[4096]{0:T(1024)S(1)}, f32[4096]{0:T(1024)}, u32[]{:S(2)}) copy-start(f32[4096]{0:T(1024)} %param.19) | copy-start | bytes 49156
  110.2 3.0 copy-start.2
  118.2 2.6 copy-start.4
  119.5 1.4 copy-start.1
  120.8 0.7 copy-start.11
  122.9 30.2 %copy-start.5 = (f32[4096]{0:T(1024)S(1)}, f32[4096]{0:T(1024)}, u32[]{:S(2)}) copy-start(f32[4096]{0:T(1024)} %param.24) | copy-start | bytes 49156
  126.8 77.6 %all-gather.10.cloned.1.call-start = ((), (), s32[]{:S(2)}) async-start(), calls=%async_computation.4 | async-start | bytes 2359296 | tf_op jit(solution)/shard_map/all_gather | solution.py:133
  155.1 1.3 copy-start.10
  155.1 1.4 copy-start.6
  155.1 442.0 %all-gather.12.cloned.1.call-start = ((), (), s32[]{:S(2)}) async-start(), calls=%async_computation.5 | async-start | bytes 83886080 | tf_op jit(solution)/shard_map/all_gather | solution.py:143
  649.0 28.9 %copy-start.8 = (f32[22]{0:T(128)S(1)}, f32[22]{0:T(128)}, u32[]{:S(2)}) copy-start(f32[22]{0:T(128)} %param.26) | copy-start | bytes 268
  649.0 28.9 %copy-start.9 = (f32[22]{0:T(128)S(1)}, f32[22]{0:T(128)}, u32[]{:S(2)}) copy-start(f32[22]{0:T(128)} %param.27) | copy-start | bytes 268
  678.6 3.1 copy-start.7
Sparse Core Ops, SparseCore 0:
  10.1 75.5 all-gather.5
  93.4 15.2 all-gather.7
  127.0 24.7 reduce-scatter.1
  155.2 49.1 all-gather.9
  205.8 391.2 all-gather.11
where the time goes:
time: 689 us; the launch traced here: 688 us
  waiting for transfers between devices  493 us (72%)
  blocking collectives  94.2 us (14%)
  matrix products  51.6 us (7%)
  local copies, waits for them, and re-layouts  18.6 us (3%)
  between operations  15.3 us (2%)
  other arithmetic  15.2 us (2%)
    all_gather x1, waiting for transfers between devices, local(): lax.all_gather(w_vocab, 'mp', axis=0, tiled=True)  393 us
    all_gather x1, waiting for transfers between devices, local(): lax.all_gather(embedded, 'dp', axis=0, tiled=True)  58.5 us
    dot_general x1, matrix products, local(): jnp.dot(all_rows, lax.all_gather(w_vocab, 'mp', axis=0, tiled=True), pref...  30.6 us
    all_gather x1, blocking collectives, local(): lax.all_gather(targets, 'dp', axis=0, tiled=True)  26.2 us
    reduce_scatter x1, waiting for transfers between devices, local(): lax.psum_scatter(jnp.dot(mixed_heads, w_out, preferred_element_type=jnp.f...  24.9 us
    unnamed x2, blocking collectives  23.6 us
    pmax x1, blocking collectives, local(): top_all = lax.pmax(row_top, 'dp')  21.3 us
    psum x1, blocking collectives, local(): summed = lax.psum((spread * jnp.exp(row_top - top_all), picked), 'dp')  17.1 us
  transfers between devices with their start and end apart: 5, of which 5 were waited for; matrix products, arithmetic and copies ran while one was open for 2% of the time, Pallas kernels for 0%

commit v1 on v0

v1 whole, which is shorter than its diff:
```python
import jax
import jax.numpy as jnp
from jax import lax
from jax.sharding import PartitionSpec as P

HEAD_DIM = 128
DOMAINS = 22
CHUNKS = 4

norm_eps = 1e-05
rope_base = 500000.0
memory_rate = 0.9
step_rate = 0.02
explore_mass = 0.005


def rotate_halves(tensor):
    full_width = tensor.shape[-1]
    half_width = full_width // 2
    frequency = jnp.power(
        jnp.float32(rope_base), -jnp.arange(half_width, dtype=jnp.float32) * 2.0 / full_width
    )
    angles = jnp.arange(tensor.shape[1], dtype=jnp.float32)[:, None] * frequency[None, :]
    cosine = jnp.cos(angles)[None, :, None, :]
    sine_part = jnp.sin(angles)[None, :, None, :]
    first_half = tensor[..., :half_width]
    second = tensor[..., half_width:]
    return jnp.concatenate(
        [first_half * cosine - second * sine_part, second * cosine + first_half * sine_part],
        axis=-1,
    )


def attend(full_rows, gain_in, w_query, w_key, w_value, seqs, seq_len):
    values = full_rows.astype(jnp.float32)
    inv_rms = lax.rsqrt(jnp.mean(values * values, axis=-1, keepdims=True) + norm_eps)
    normed = (values * inv_rms * gain_in).astype(jnp.bfloat16)
    local_heads = w_query.shape[1] // HEAD_DIM
    local_groups = w_key.shape[1] // HEAD_DIM
    group_size = local_heads // local_groups
    query = jnp.dot(normed, w_query, preferred_element_type=jnp.float32)
    key = jnp.dot(normed, w_key, preferred_element_type=jnp.float32)
    value = jnp.dot(normed, w_value, preferred_element_type=jnp.float32).astype(jnp.bfloat16)
    query = rotate_halves(query.reshape(seqs, seq_len, local_heads, HEAD_DIM))
    key = rotate_halves(key.reshape(seqs, seq_len, local_groups, HEAD_DIM))
    query = query.astype(jnp.bfloat16).reshape(seqs, seq_len, local_groups, group_size, HEAD_DIM)
    key = key.astype(jnp.bfloat16)
    value = value.reshape(seqs, seq_len, local_groups, HEAD_DIM)
    scores = jnp.einsum(
        "sqgre,skge->sgrqk", query, key, preferred_element_type=jnp.float32
    ) * HEAD_DIM ** (-0.5)
    causal = jnp.arange(seq_len)[:, None] >= jnp.arange(seq_len)[None, :]
    scores = jnp.where(causal, scores, -jnp.inf)
    weights = jax.nn.softmax(scores, axis=-1).astype(jnp.bfloat16)
    mixed = jnp.einsum("sgrqk,skge->sqgre", weights, value, preferred_element_type=jnp.float32)
    return mixed.astype(jnp.bfloat16).reshape(seqs * seq_len, local_heads * HEAD_DIM)


def local(
    embedded,
    targets,
    labels,
    counts,
    destinations,
    gain_in,
    w_query,
    w_key,
    w_value,
    w_out,
    gain_out,
    w_vocab,
    prev_probs,
    log_weights,
):
    dp = lax.axis_size("dp")
    mp = lax.axis_size("mp")
    data_index = lax.axis_index("dp")
    model_index = lax.axis_index("mp")
    chip = model_index // 2
    core = model_index % 2
    slots, seq_len, width = embedded.shape
    sequences = dp * slots // 2
    tokens = sequences * seq_len
    sibling = [(i, i ^ 1) for i in range(mp)]
    vocab_local = w_vocab.shape[1]
    columns = vocab_local // 2

    own_columns = lax.dynamic_slice_in_dim(w_vocab, core * columns, columns, 1)
    given_columns = lax.dynamic_slice_in_dim(w_vocab, (1 - core) * columns, columns, 1)
    taken_columns = lax.ppermute(given_columns, "mp", sibling)

    packed = jnp.concatenate([targets, labels[:, None], destinations[:, None]], axis=1)
    packed_all = lax.all_gather(packed, "dp", axis=0, tiled=True)
    slot_ids = jnp.arange(dp * slots, dtype=jnp.int32)
    is_live = slot_ids % slots < counts[slot_ids // slots]
    wanted = jnp.arange(sequences, dtype=jnp.int32)
    chosen = (packed_all[:, seq_len + 1][None, :] == wanted[:, None]) & is_live[None, :]
    source = jnp.sum(jnp.where(chosen, slot_ids[None, :], 0), axis=1).astype(jnp.int32)
    picked_ints = jnp.sum(jnp.where(chosen[:, :, None], packed_all[None], 0), axis=1)
    seq_targets = picked_ints[:, :seq_len]
    seq_labels = picked_ints[:, seq_len]

    flat = embedded.reshape(slots * seq_len, width)
    full_rows = lax.all_gather(flat, "mp", axis=1, tiled=True)
    mixed = attend(full_rows, gain_in, w_query, w_key, w_value, slots, seq_len)
    partial = jnp.dot(mixed, w_out, preferred_element_type=jnp.float32).astype(jnp.bfloat16)
    update = lax.psum_scatter(partial, "mp", scatter_dimension=1, tiled=True)
    hidden = flat.astype(jnp.float32) + update.astype(jnp.float32)
    squares = lax.psum(jnp.sum(hidden * hidden, axis=-1, keepdims=True), "mp") / (width * mp)
    gain_part = lax.dynamic_slice_in_dim(gain_out, model_index * width, width, 0)
    final = (hidden * lax.rsqrt(squares + norm_eps) * gain_part).astype(jnp.bfloat16)
    everyone = lax.all_gather(final.reshape(slots, seq_len, width), "dp", axis=0, tiled=True)

    chips = mp // 2
    seq_part = sequences // chips
    order = jnp.roll(source, -chip * seq_part)
    rows = jnp.concatenate(
        [lax.dynamic_index_in_dim(everyone, order[i], 0, keepdims=True) for i in range(sequences)]
    ).reshape(tokens, width)
    their_rows = lax.ppermute(rows, "mp", sibling)
    part = tokens // chips
    goals = jnp.roll(seq_targets, -chip * seq_part, axis=0)[:seq_part].reshape(part)
    goals = goals - (data_index * vocab_local + core * columns)

    def product(lhs, other, start, size):
        return jnp.dot(
            lhs, own_columns[:, start : start + size], preferred_element_type=jnp.float32
        ) + jnp.dot(
            other, taken_columns[:, start : start + size], preferred_element_type=jnp.float32
        )

    size = columns // CHUNKS
    arrived = []
    for i in range(CHUNKS):
        hops = []
        for hop in range(1, chips):
            there = slice(hop * part, (hop + 1) * part)
            outgoing = product(rows[there], their_rows[there], i * size, size)
            across = [(j, (j + 2 * hop) % mp) for j in range(mp)]
            hops.append(lax.ppermute(outgoing.astype(jnp.bfloat16), "mp", across))
        arrived.append(hops)
    tops, spreads, picks = [], [], []
    for i in range(CHUNKS):
        logits = product(rows[:part], their_rows[:part], i * size, size)
        for piece in arrived[i]:
            logits = logits + piece.astype(jnp.float32)
        top = jnp.max(logits, axis=1)
        tops.append(top)
        spreads.append(jnp.sum(jnp.exp(logits - top[:, None]), axis=1))
        ids = i * size + jnp.arange(size, dtype=jnp.int32)
        picks.append(jnp.sum(jnp.where(ids[None, :] == goals[:, None], logits, 0.0), axis=1))
    stats = jnp.stack(tops + spreads + picks)
    stats_all = lax.all_gather(stats, ("dp", "mp"), axis=0, tiled=False)
    stats_all = stats_all.reshape(dp, chips, 2, 3, CHUNKS, part)
    top_all = jnp.max(stats_all[:, :, :, 0], axis=(0, 2, 3))
    scale = jnp.exp(stats_all[:, :, :, 0] - top_all[None, :, None, None])
    spread_all = jnp.sum(stats_all[:, :, :, 1] * scale, axis=(0, 2, 3))
    picked_all = jnp.sum(stats_all[:, :, :, 2], axis=(0, 2, 3))
    losses = (top_all + jnp.log(spread_all) - picked_all).reshape(tokens)

    block = tokens // (dp * mp)
    own_loss = lax.dynamic_slice_in_dim(
        losses, (data_index * mp + model_index) * block, block, 0
    )
    domains = jnp.arange(DOMAINS, dtype=jnp.int32)
    member = (seq_labels[:, None] == domains[None, :]).astype(jnp.float32)
    per_sequence = jnp.sum(losses.reshape(sequences, seq_len), axis=1)
    loss_sums = jnp.sum(member * per_sequence[:, None], axis=0)
    token_tally = jnp.sum(member, axis=0) * seq_len
    reward = loss_sums / jnp.maximum(token_tally, 1.0) / prev_probs
    new_weights = memory_rate * log_weights + (1.0 - memory_rate) * reward
    probs = (1.0 - DOMAINS * explore_mass) * jax.nn.softmax(step_rate * new_weights) + explore_mass
    return (own_loss, new_weights, probs)


def solution(mesh):
    placed = (
        P("dp", None, "mp"),
        P("dp", None),
        P("dp"),
        P(),
        P("dp"),
        P(),
        P(None, "mp"),
        P(None, "mp"),
        P(None, "mp"),
        P("mp", None),
        P(),
        P("mp", "dp"),
        P(),
        P(),
    )
    return jax.shard_map(
        local, mesh=mesh, in_specs=placed, out_specs=(P(("dp", "mp")), P(), P()), check_vma=False
    )
```

time: 689 us -> 358 us (0.52)
  waiting for transfers between devices: 493 us -> 135 us
  between operations: 15.3 us -> 44.7 us
  blocking collectives: 94.2 us -> 75.1 us
  local copies, waits for them, and re-layouts: 18.6 us -> 28.4 us
    all_gather x4 -> x2, waiting for transfers between devices: 467 us -> 32.9 us  [the longest x1 26.7 us: local(): full_rows = lax.all_gather(flat, 'mp', axis=1, tiled=True)]
    ppermute x0 -> x6, waiting for transfers between devices: none -> 70.8 us  [the longest x4 70.8 us: local(): hops.append(lax.ppermute(outgoing.astype(jnp.bfloat16), 'mp', across))]
    all_gather x1 -> x2, blocking collectives: 26.2 us -> 69.3 us  [the longest x1 42.3 us: local(): stats_all = lax.all_gather(stats, ('dp', 'mp'), axis=0, tiled=False)]
    unnamed x2 -> x0, blocking collectives: 23.6 us -> none
    pmax x1 -> x0, blocking collectives: 21.3 us -> none  [local(): top_all = lax.pmax(row_top, 'dp')]
    psum x2 -> x1, blocking collectives: 23.1 us -> 5.76 us  [local(): lax.psum(jnp.sum(hidden * hidden, axis=-1, keepdims=True), 'mp')]
    dot_general x3 -> x0, local copies, waits for them, and re-layouts: 11.4 us -> none  [the longest x1 6.49 us: local(): jnp.dot(normed, w_query, preferred_element_type=jnp.float32)]
    unnamed x33 -> x64, local copies, waits for them, and re-layouts: 4.78 us -> 13.8 us
  transfers between devices with their start and end apart: 5 -> 9, of which waited for: 5 -> 7; matrix products, arithmetic and copies ran while one was open for 2% -> 17% of each run, Pallas kernels for 0% -> 0%
where the time goes in v1:
time: 358 us; the launch traced here: 356 us
  waiting for transfers between devices  135 us (38%)
  blocking collectives  75.1 us (21%)
  matrix products  54 us (15%)
  between operations  44.7 us (12%)
  local copies, waits for them, and re-layouts  28.4 us (8%)
  other arithmetic  14.8 us (4%)
  starting transfers between devices  4.5 us (1%)
    ppermute x4, waiting for transfers between devices, local(): hops.append(lax.ppermute(outgoing.astype(jnp.bfloat16), 'mp', across))  70.8 us
    all_gather x1, blocking collectives, local(): stats_all = lax.all_gather(stats, ('dp', 'mp'), axis=0, tiled=False)  42.3 us
    reduce_scatter x1, waiting for transfers between devices, local(): update = lax.psum_scatter(partial, 'mp', scatter_dimension=1, tiled=True)  30.5 us
    all_gather x1, blocking collectives, local(): packed_all = lax.all_gather(packed, 'dp', axis=0, tiled=True)  27 us
    all_gather x1, waiting for transfers between devices, local(): full_rows = lax.all_gather(flat, 'mp', axis=1, tiled=True)  26.7 us
    dot_general x8, matrix products, product(): jnp.dot(other, taken_columns[:, start:start + size], preferred_element_ty...  23.8 us
    dot_general x8, matrix products, product(): jnp.dot(lhs, own_columns[:, start:start + size], preferred_element_type=j...  17 us
    unnamed x64, local copies, waits for them, and re-layouts  13.8 us
  transfers between devices with their start and end apart: 9, of which 7 were waited for; matrix products, arithmetic and copies ran while one was open for 17% of the time, Pallas kernels for 0%

profile of v1, /device:TPU:0, one launch (start us, length us, event | category | flops | bytes accessed | tf_op | source)
XLA Modules:
  0.0 356.4 jit_solution(2570674552904106741)
XLA Ops:
  8.2 26.7 %all-gather.6.cloned.1.call-done = bf16[256,4096]{1,0:T(8,128)(2,1)} async-done(((bf16[256,1024]{1,0:T(8,128)(2,1)}), bf16[256,4096]{1,0:T(8,128)(2,1)}) %all-gather.6.cloned.1.call-update) | async-done | bytes 2097168 | tf_op jit(solution)/shard_map/all_gather | solution.py:104
  34.9 2.2 fusion.1
  37.1 3.5 fusion.113
  43.7 3.0 convolution_convert_fusion.2
  48.4 4.8 %convolution_convert_fusion = bf16[256,4096]{1,0:T(8,128)(2,1)} fusion(bf16[256,512]{1,0:T(8,128)(2,1)S(1)} %reshape.229, bf16[512,4096]{1,0:T(8,128)(2,1)} %param.23), kind=kOutput, calls=%fused_computation.4 | convolution fusion | flops 1074790400 | bytes 6553600 | tf_op jit(solution)/shard_map/dot_general | solution.py:106
  54.0 30.5 %reduce-scatter.2.cloned.1.call-done = bf16[256,1024]{1,0:T(8,128)(2,1)} async-done(((bf16[256,4096]{1,0:T(8,128)(2,1)}), bf16[256,1024]{1,0:T(8,128)(2,1)}) %reduce-scatter.2.cloned.1.call-update) | async-done | bytes 524304 | tf_op jit(solution)/shard_map/reduce_scatter | solution.py:107
  85.8 5.8 %psum.7 = f32[256,1]{0,1:T(1,128)S(1)} all-reduce(f32[256,1]{0,1:T(1,128)S(1)} %bitcast.145), channel_id=1, replica_groups=mesh['dp'=8,'mp'=4] {'mp'}, use_global_device_ids=true, to_apply=%region_5.6 | all-reduce | flops 256 | bytes 2048 | tf_op jit(solution)/shard_map/psum | solution.py:109
  91.6 2.0 multiply_convert_fusion
  93.7 7.7 %constant_dynamic-slice_fusion = bf16[1024,4096]{1,0:T(8,128)(2,1)} fusion(bf16[1024,8192]{1,0:T(8,128)(2,1)} %param.25, s32[]{:T(128)S(6)} %select_n.174), kind=kLoop, calls=%fused_computation.149 | loop fusion | bytes 16777220 | tf_op jit(solution)/shard_map/dynamic_slice | solution.py:89
  101.7 27.0 %all-gather.1 = s32[8,4,66]{2,1,0:T(4,128)S(1)} all-gather(s32[1,4,66]{2,1,0:T(4,128)S(1)} %add_bitcast_fusion), channel_id=1, replica_groups=mesh['dp'=8,'mp'=4] {'dp'}, dimensions={0}, use_global_device_ids=true | all-gather | bytes 9504 | tf_op jit(solution)/shard_map/all_gather | solution.py:93
  161.4 6.2 %all-gather.8.cloned.1.call-done = bf16[32,64,1024]{2,1,0:T(8,128)(2,1)} async-done(((bf16[4,64,1024]{2,1,0:T(8,128)(2,1)}), bf16[32,64,1024]{2,1,0:T(8,128)(2,1)}) %all-gather.8.cloned.1.call-update) | async-done | bytes 4194320 | tf_op jit(solution)/shard_map/all_gather | solution.py:112
  181.6 3.0 fusion.32
  184.6 3.0 fusion.34
  187.6 3.0 fusion.28
  190.6 2.8 fusion.30
  198.7 2.9 add_convert_fusion.3
  201.6 1.5 collective-permute-start.2
  203.1 2.9 add_convert_fusion.2
  206.6 3.1 add_convert_fusion.1
  209.7 1.5 collective-permute-start.4
  211.2 2.9 add_convert_fusion
  214.8 12.9 %collective-permute-done.2 = bf16[512,1024]{1,0:T(8,128)(2,1)S(1)} collective-permute-done((bf16[512,1024]{1,0:T(8,128)(2,1)S(1)}, bf16[512,1024]{1,0:T(8,128)(2,1)S(1)}, u32[]{:S(2)}, u32[]{:S(2)}) %collective-permute-start.2) | collective-permute-done | bytes 1048608 | tf_op jit(solution)/shard_map/ppermute | solution.py:140
  227.7 3.0 fusion.124
  230.7 19.5 %collective-permute-done.3 = bf16[512,1024]{1,0:T(8,128)(2,1)S(1)} collective-permute-done((bf16[512,1024]{1,0:T(8,128)(2,1)S(1)}, bf16[512,1024]{1,0:T(8,128)(2,1)S(1)}, u32[]{:S(2)}, u32[]{:S(2)}) %collective-permute-start.3) | collective-permute-done | bytes 1048608 | tf_op jit(solution)/shard_map/ppermute | solution.py:140
  250.2 3.0 fusion.125
  253.2 19.5 %collective-permute-done.4 = bf16[512,1024]{1,0:T(8,128)(2,1)S(1)} collective-permute-done((bf16[512,1024]{1,0:T(8,128)(2,1)S(1)}, bf16[512,1024]{1,0:T(8,128)(2,1)S(1)}, u32[]{:S(2)}, u32[]{:S(2)}) %collective-permute-start.4) | collective-permute-done | bytes 1048608 | tf_op jit(solution)/shard_map/ppermute | solution.py:140
  272.6 3.0 fusion.126
  275.7 19.0 %collective-permute-done.5 = bf16[512,1024]{1,0:T(8,128)(2,1)S(1)} collective-permute-done((bf16[512,1024]{1,0:T(8,128)(2,1)S(1)}, bf16[512,1024]{1,0:T(8,128)(2,1)S(1)}, u32[]{:S(2)}, u32[]{:S(2)}) %collective-permute-start.5) | collective-permute-done | bytes 1048608 | tf_op jit(solution)/shard_map/ppermute | solution.py:140
  294.6 3.0 fusion.127
  297.6 2.5 select_reduce_fusion
  300.3 42.3 %all-gather.2 = f32[32,12,512]{2,1,0:T(8,128)S(1)} all-gather(f32[1,12,512]{2,1,0:T(8,128)S(1)} %bitcast.120), channel_id=2, replica_groups=mesh['dp'=8,'mp'=4] {'dp','mp'}, dimensions={0}, use_global_device_ids=true | all-gather | bytes 811008 | tf_op jit(solution)/shard_map/all_gather | solution.py:153
  347.4 1.9 multiply_add_fusion
  (134 shorter events, 36.2 us)
Async XLA Ops:
  7.2 34.2 %copy-start = (bf16[4096,256]{1,0:T(8,128)(2,1)S(1)}, bf16[4096,256]{1,0:T(8,128)(2,1)}, u32[]{:S(2)}) copy-start(bf16[4096,256]{1,0:T(8,128)(2,1)} %param.21) | copy-start | bytes 6291460
  7.2 29.9 %copy-start.13 = (f32[4096]{0:T(1024)S(1)}, f32[4096]{0:T(1024)}, u32[]{:S(2)}) copy-start(f32[4096]{0:T(1024)} %param.19) | copy-start | bytes 49156
  7.2 27.7 %all-gather.6.cloned.1.call-start = ((), (), s32[]{:S(2)}) async-start(), calls=%async_computation.1 | async-start | bytes 2621440 | tf_op jit(solution)/shard_map/all_gather | solution.py:104
  7.9 76.6 %reduce-scatter.2.cloned.1.call-start = ((), (), s32[]{:S(2)}) async-start(), calls=%async_computation.2 | async-start | bytes 2621440 | tf_op jit(solution)/shard_map/reduce_scatter | solution.py:107
  34.9 2.3 copy-start.5
  40.8 1.6 copy-start.6
  53.2 31.3 %copy-start.3 = (bf16[4,64,1024]{2,1,0:T(8,128)(2,1)S(1)}, bf16[4,64,1024]{2,1,0:T(8,128)(2,1)}, u32[]{:S(2)}) copy-start(bf16[4,64,1024]{2,1,0:T(8,128)(2,1)} %param.14) | copy-start | bytes 1572868
  53.2 114.4 %all-gather.8.cloned.1.call-start = ((), (), s32[]{:S(2)}) async-start(), calls=%async_computation.3 | async-start | bytes 4718592 | tf_op jit(solution)/shard_map/all_gather | solution.py:112
  93.7 7.8 %copy-start.9 = (s32[4]{0:T(128)S(1)}, s32[4]{0:T(128)}, u32[]{:S(2)}) copy-start(s32[4]{0:T(128)} %param.18) | copy-start | bytes 52
  93.7 7.9 %copy-start.10 = (s32[4]{0:T(128)S(1)}, s32[4]{0:T(128)}, u32[]{:S(2)}) copy-start(s32[4]{0:T(128)} %param.16) | copy-start | bytes 52
  93.7 7.9 %copy-start.7 = (s32[4,64]{1,0:T(4,128)S(1)}, s32[4,64]{1,0:T(4,128)}, u32[]{:S(2)}) copy-start(s32[4,64]{1,0:T(4,128)} %param.15) | copy-start | bytes 3076
  93.7 35.2 %copy-start.2 = (s32[8]{0:T(128)S(1)}, s32[8]{0:T(128)}, u32[]{:S(2)}) copy-start(s32[8]{0:T(128)} %param.17) | copy-start | bytes 100
  101.5 97.2 %collective-permute-start.1 = (bf16[1024,4096]{1,0:T(8,128)(2,1)}, bf16[1024,4096]{1,0:T(8,128)(2,1)}, u32[]{:S(2)}, u32[]{:S(2)}) collective-permute-start(bf16[1024,4096]{1,0:T(8,128)(2,1)} %constant_dynamic-slice_fusion), channel_id=1, source_target_pairs={{0,1},{1,0},{2,3},{3,2},{4,5},{5,4},{6,7},{7,6},{8,9},{9,8},{10,11... | collective-permute-start | bytes 25165832 | tf_op jit(solution)/shard_map/ppermute | solution.py:90
  167.6 13.5 %copy-start.4 = (bf16[32,64,1024]{2,1,0:T(8,128)(2,1)S(1)}, bf16[32,64,1024]{2,1,0:T(8,128)(2,1)}, u32[]{:S(2)}) copy-start(bf16[32,64,1024]{2,1,0:T(8,128)(2,1)} %all-gather.8.cloned.1.call-done) | copy-start | bytes 12582916
  181.2 12.3 %slice-start = ((s8[16777216]{0:T(1024)(128)(4,1)}), s8[4194304]{0:T(1024)(128)(4,1)S(1)}, s32[]{:S(2)}) async-start(s8[16777216]{0:T(1024)(128)(4,1)} %bitcast.111), calls=%async_computation.4 | async-start | bytes 8388608
  181.3 17.4 %collective-permute-start = (bf16[1024,1024]{1,0:T(8,128)(2,1)S(1)}, bf16[1024,1024]{1,0:T(8,128)(2,1)S(1)}, u32[]{:S(2)}, u32[]{:S(2)}) collective-permute-start(bf16[1024,1024]{1,0:T(8,128)(2,1)S(1)} %bitcast.144), channel_id=1, source_target_pairs={{0,1},{1,0},{2,3},{3,2},{4,5},{5,4},{6,7},{7,6},{8,9},{9,8},{10,11... | collective-permute-start | bytes 6291464 | tf_op jit(solution)/shard_map/ppermute | solution.py:120
  181.6 11.9 %slice-start.1 = ((s8[16777216]{0:T(1024)(128)(4,1)}), s8[4194304]{0:T(1024)(128)(4,1)S(1)}, s32[]{:S(2)}) async-start(s8[16777216]{0:T(1024)(128)(4,1)} %bitcast.111), calls=%async_computation.5 | async-start | bytes 8388608
  184.6 8.9 %slice-start.2 = ((s8[16777216]{0:T(1024)(128)(4,1)}), s8[4194304]{0:T(1024)(128)(4,1)S(1)}, s32[]{:S(2)}) async-start(s8[16777216]{0:T(1024)(128)(4,1)} %bitcast.111), calls=%async_computation.6 | async-start | bytes 8388608
  187.6 5.9 %slice-start.3 = ((s8[16777216]{0:T(1024)(128)(4,1)}), s8[4194304]{0:T(1024)(128)(4,1)S(1)}, s32[]{:S(2)}) async-start(s8[16777216]{0:T(1024)(128)(4,1)} %bitcast.111), calls=%async_computation.7 | async-start | bytes 8388608
  201.6 26.1 %collective-permute-start.2 = (bf16[512,1024]{1,0:T(8,128)(2,1)S(1)}, bf16[512,1024]{1,0:T(8,128)(2,1)S(1)}, u32[]{:S(2)}, u32[]{:S(2)}) collective-permute-start(bf16[512,1024]{1,0:T(8,128)(2,1)S(1)} %add_convert_fusion.3), channel_id=1, source_target_pairs={{0,2},{1,3},{2,0},{3,1},{4,6},{5,7},{6,4},{7,5},{8,10},{9,11},{10,... | collective-permute-start | bytes 3145736 | tf_op jit(solution)/shard_map/ppermute | solution.py:140
  206.0 44.2 %collective-permute-start.3 = (bf16[512,1024]{1,0:T(8,128)(2,1)S(1)}, bf16[512,1024]{1,0:T(8,128)(2,1)S(1)}, u32[]{:S(2)}, u32[]{:S(2)}) collective-permute-start(bf16[512,1024]{1,0:T(8,128)(2,1)S(1)} %add_convert_fusion.2), channel_id=1, source_target_pairs={{0,2},{1,3},{2,0},{3,1},{4,6},{5,7},{6,4},{7,5},{8,10},{9,11},{10,... | collective-permute-start | bytes 3145736 | tf_op jit(solution)/shard_map/ppermute | solution.py:140
  209.7 62.9 %collective-permute-start.4 = (bf16[512,1024]{1,0:T(8,128)(2,1)S(1)}, bf16[512,1024]{1,0:T(8,128)(2,1)S(1)}, u32[]{:S(2)}, u32[]{:S(2)}) collective-permute-start(bf16[512,1024]{1,0:T(8,128)(2,1)S(1)} %add_convert_fusion.1), channel_id=1, source_target_pairs={{0,2},{1,3},{2,0},{3,1},{4,6},{5,7},{6,4},{7,5},{8,10},{9,11},{10,... | collective-permute-start | bytes 3145736 | tf_op jit(solution)/shard_map/ppermute | solution.py:140
  214.1 80.5 %collective-permute-start.5 = (bf16[512,1024]{1,0:T(8,128)(2,1)S(1)}, bf16[512,1024]{1,0:T(8,128)(2,1)S(1)}, u32[]{:S(2)}, u32[]{:S(2)}) collective-permute-start(bf16[512,1024]{1,0:T(8,128)(2,1)S(1)} %add_convert_fusion), channel_id=1, source_target_pairs={{0,2},{1,3},{2,0},{3,1},{4,6},{5,7},{6,4},{7,5},{8,10},{9,11},{10,... | collective-permute-start | bytes 3145736 | tf_op jit(solution)/shard_map/ppermute | solution.py:140
  300.2 49.6 %copy-start.1 = (bf16[4096,256]{1,0:T(8,128)(2,1)S(1)}, bf16[4096,256]{1,0:T(8,128)(2,1)}, u32[]{:S(2)}) copy-start(bf16[4096,256]{1,0:T(8,128)(2,1)} %param.21) | copy-start | bytes 6291460
  342.5 2.9 copy-start.11
  342.5 2.9 copy-start.12
  346.1 3.8 %copy-start.8 = (f32[22]{0:T(128)}, f32[22]{0:T(128)S(1)}, u32[]{:S(2)}) copy-start(f32[22]{0:T(128)S(1)} %get-tuple-element.22) | copy-start | bytes 268
Sparse Core Ops, SparseCore 0:
  9.6 25.2 all-gather.5
  53.4 31.1 reduce-scatter.1
  93.8 73.7 all-gather.7

commit v2 on v1

v2 whole, which is shorter than its diff:
```python
import functools

import jax
import jax.numpy as jnp
from jax import lax
from jax.experimental import pallas as pl
from jax.experimental.pallas import tpu as pltpu
from jax.sharding import PartitionSpec as P

HEAD_DIM = 128
DOMAINS = 22
PIECES = 4
MESH = pl.DeviceIdType.MESH
VMEM = pl.BlockSpec(memory_space=pltpu.VMEM)

norm_eps = 1e-05
rope_base = 500000.0
memory_rate = 0.9
step_rate = 0.02
explore_mass = 0.005


def rotate_halves(tensor):
    full_width = tensor.shape[-1]
    half_width = full_width // 2
    frequency = jnp.power(
        jnp.float32(rope_base), -jnp.arange(half_width, dtype=jnp.float32) * 2.0 / full_width
    )
    angles = jnp.arange(tensor.shape[1], dtype=jnp.float32)[:, None] * frequency[None, :]
    cosine = jnp.cos(angles)[None, :, None, :]
    sine_part = jnp.sin(angles)[None, :, None, :]
    first_half = tensor[..., :half_width]
    second = tensor[..., half_width:]
    return jnp.concatenate(
        [first_half * cosine - second * sine_part, second * cosine + first_half * sine_part],
        axis=-1,
    )


def attend(full_rows, gain_in, w_query, w_key, w_value, seqs, seq_len):
    values = full_rows.astype(jnp.float32)
    inv_rms = lax.rsqrt(jnp.mean(values * values, axis=-1, keepdims=True) + norm_eps)
    normed = (values * inv_rms * gain_in).astype(jnp.bfloat16)
    local_heads = w_query.shape[1] // HEAD_DIM
    local_groups = w_key.shape[1] // HEAD_DIM
    group_size = local_heads // local_groups
    query = jnp.dot(normed, w_query, preferred_element_type=jnp.float32)
    key = jnp.dot(normed, w_key, preferred_element_type=jnp.float32)
    value = jnp.dot(normed, w_value, preferred_element_type=jnp.float32).astype(jnp.bfloat16)
    query = rotate_halves(query.reshape(seqs, seq_len, local_heads, HEAD_DIM))
    key = rotate_halves(key.reshape(seqs, seq_len, local_groups, HEAD_DIM))
    query = query.astype(jnp.bfloat16).reshape(seqs, seq_len, local_groups, group_size, HEAD_DIM)
    key = key.astype(jnp.bfloat16)
    value = value.reshape(seqs, seq_len, local_groups, HEAD_DIM)
    scores = jnp.einsum(
        "sqgre,skge->sgrqk", query, key, preferred_element_type=jnp.float32
    ) * HEAD_DIM ** (-0.5)
    causal = jnp.arange(seq_len)[:, None] >= jnp.arange(seq_len)[None, :]
    scores = jnp.where(causal, scores, -jnp.inf)
    weights = jax.nn.softmax(scores, axis=-1).astype(jnp.bfloat16)
    mixed = jnp.einsum("sgrqk,skge->sqgre", weights, value, preferred_element_type=jnp.float32)
    return mixed.astype(jnp.bfloat16).reshape(seqs * seq_len, local_heads * HEAD_DIM)


def remote(src, dst, send_sem, recv_sem, device):
    return pltpu.make_async_remote_copy(
        src_ref=src,
        dst_ref=dst,
        send_sem=send_sem,
        recv_sem=recv_sem,
        device_id=device,
        device_id_type=MESH,
    )


def greet(peers):
    barrier = pltpu.get_barrier_semaphore()
    for peer in peers:
        pl.semaphore_signal(barrier, inc=1, device_id=peer, device_id_type=MESH)
    pl.semaphore_wait(barrier, len(peers))


def features_kernel(
    dp, mp, x_ref, ints_ref, full_ref, all_ints_ref,
    across_send, across_recv, side_send, side_recv, int_send, int_recv, local_sem,
):
    d, m = lax.axis_index("dp"), lax.axis_index("mp")
    chips = mp // 2
    chip, core = m // 2, m % 2
    sibling = (d, chip * 2 + (1 - core))
    rows, width = x_ref.shape
    size = rows // PIECES
    far = [(d, lax.rem(chip + hop, chips) * 2 + core) for hop in range(1, chips)]
    around = [(lax.rem(d + k, dp), m) for k in range(1, dp)]
    greet([sibling] + far + around)

    def place(block, piece):
        start = pl.multiple_of(block * width, width)
        return full_ref.at[pl.ds(piece * size, size), pl.ds(start, width)]

    waits = []
    for piece in range(PIECES):
        for hop in range(1, chips):
            copy = remote(
                x_ref.at[pl.ds(piece * size, size)], place(m, piece),
                across_send.at[hop - 1, piece], across_recv.at[hop - 1, piece], far[hop - 1],
            )
            copy.start()
            waits.append(copy)
    sides = []
    for piece in range(PIECES):
        copy = remote(
            x_ref.at[pl.ds(piece * size, size)], place(m, piece),
            side_send.at[0, piece], side_recv.at[0, piece], sibling,
        )
        copy.start()
        sides.append(copy)
    ints = []
    for k in range(1, dp):
        copy = remote(
            ints_ref, all_ints_ref.at[d], int_send.at[k - 1], int_recv.at[k - 1], around[k - 1]
        )
        copy.start()
        ints.append(copy)
    locals_ = [
        pltpu.make_async_copy(ints_ref, all_ints_ref.at[d], local_sem.at[0]),
        pltpu.make_async_copy(
            x_ref, full_ref.at[:, pl.ds(pl.multiple_of(m * width, width), width)], local_sem.at[1]
        ),
    ]
    for copy in locals_:
        copy.start()
    at = 0
    for piece in range(PIECES):
        for hop in range(1, chips):
            waits[at].wait_recv()
            at += 1
            origin = lax.rem(chip + chips - hop, chips) * 2 + core
            copy = remote(
                place(origin, piece), place(origin, piece),
                side_send.at[hop, piece], side_recv.at[hop, piece], sibling,
            )
            copy.start()
            sides.append(copy)
    for copy in waits:
        copy.wait_send()
    for copy in sides + ints + locals_:
        copy.wait()


def gather_features(flat, ints, dp, mp):
    rows, width = flat.shape
    chips = mp // 2
    dma = pltpu.SemaphoreType.DMA
    return pl.pallas_call(
        functools.partial(features_kernel, dp, mp),
        out_shape=(
            jax.ShapeDtypeStruct((rows, width * mp), flat.dtype),
            jax.ShapeDtypeStruct((dp,) + ints.shape, ints.dtype),
        ),
        in_specs=[VMEM] * 2,
        out_specs=(VMEM, VMEM),
        scratch_shapes=[
            dma((chips - 1, PIECES)), dma((chips - 1, PIECES)),
            dma((chips, PIECES)), dma((chips, PIECES)),
            dma((dp - 1,)), dma((dp - 1,)), dma((2,)),
        ],
        compiler_params=pltpu.CompilerParams(collective_id=0, has_side_effects=True),
        name="features",
    )(flat, ints)


def output_kernel(
    mp, mixed_ref, w_ref, own_ref, gain_ref, final_ref,
    side_out, side_in, far_out, far_in, kept, total, square_out, square_in,
    side_send, side_recv, far_send, far_recv, square_send, square_recv,
):
    d, m = lax.axis_index("dp"), lax.axis_index("mp")
    chips = mp // 2
    chip, core = m // 2, m % 2
    sibling = (d, chip * 2 + (1 - core))
    rows, width = own_ref.shape
    size = rows // PIECES
    peers = [(d, lax.rem(m + k, mp)) for k in range(1, mp)]
    greet(peers)
    hops = list(range(1, chips)) + [0]
    target = [lax.rem(chip + hop, chips) for hop in range(chips)]

    def product(block):
        start = pl.multiple_of(block * width, width)
        return jnp.dot(
            mixed_ref[...], w_ref[:, pl.ds(start, width)], preferred_element_type=jnp.float32
        )

    def cut(piece):
        return pl.ds(piece * size, size)

    sides = {}
    for hop in hops:
        side_out[hop] = product(target[hop] * 2 + (1 - core)).astype(jnp.bfloat16)
        for piece in range(PIECES):
            sides[hop, piece] = remote(
                side_out.at[hop, cut(piece)], side_in.at[hop, cut(piece)],
                side_send.at[hop, piece], side_recv.at[hop, piece], sibling,
            )
            sides[hop, piece].start()
    for hop in hops:
        kept[hop] = product(target[hop] * 2 + core)
    fars = {}
    for piece in range(PIECES):
        for hop in range(1, chips):
            sides[hop, piece].wait_recv()
            far_out[hop - 1, cut(piece)] = (
                kept[hop, cut(piece)] + side_in[hop, cut(piece)].astype(jnp.float32)
            ).astype(jnp.bfloat16)
            fars[hop, piece] = remote(
                far_out.at[hop - 1, cut(piece)], far_in.at[hop - 1, cut(piece)],
                far_send.at[hop - 1, piece], far_recv.at[hop - 1, piece],
                (d, target[hop] * 2 + core),
            )
            fars[hop, piece].start()
    for piece in range(PIECES):
        sides[0, piece].wait_recv()
        value = kept[0, cut(piece)] + side_in[0, cut(piece)].astype(jnp.float32)
        for hop in range(1, chips):
            fars[hop, piece].wait_recv()
            value = value + far_in[hop - 1, cut(piece)].astype(jnp.float32)
        total[cut(piece)] = value + own_ref[cut(piece)].astype(jnp.float32)
    hidden = total[...]
    squares = jnp.sum(hidden * hidden, axis=1, keepdims=True)
    square_out[...] = jnp.transpose(jnp.broadcast_to(squares, (rows, 128)))[:8]
    swaps = []
    for k in range(1, mp):
        copy = remote(
            square_out, square_in.at[k - 1],
            square_send.at[k - 1], square_recv.at[k - 1], peers[k - 1],
        )
        copy.start()
        swaps.append(copy)
    for copy in swaps:
        copy.wait()
    summed = square_out[...]
    for k in range(mp - 1):
        summed = summed + square_in[k]
    inverse = lax.rsqrt(summed / (width * mp) + norm_eps)
    inverse = jnp.transpose(jnp.concatenate([inverse] * 16, axis=0))[:, :1]
    final_ref[...] = (total[...] * inverse * gain_ref[...]).astype(final_ref.dtype)
    for copy in list(sides.values()) + list(fars.values()):
        copy.wait_send()


def project_output(mixed, w_out, own, gain_part, mp):
    rows, width = own.shape
    chips = mp // 2
    dma = pltpu.SemaphoreType.DMA
    half = jnp.bfloat16
    return pl.pallas_call(
        functools.partial(output_kernel, mp),
        out_shape=jax.ShapeDtypeStruct(own.shape, half),
        in_specs=[VMEM] * 4,
        out_specs=VMEM,
        scratch_shapes=[
            pltpu.VMEM((chips, rows, width), half),
            pltpu.VMEM((chips, rows, width), half),
            pltpu.VMEM((chips - 1, rows, width), half),
            pltpu.VMEM((chips - 1, rows, width), half),
            pltpu.VMEM((chips, rows, width), jnp.float32),
            pltpu.VMEM((rows, width), jnp.float32),
            pltpu.VMEM((8, rows), jnp.float32),
            pltpu.VMEM((mp - 1, 8, rows), jnp.float32),
            dma((chips, PIECES)), dma((chips, PIECES)),
            dma((chips - 1, PIECES)), dma((chips - 1, PIECES)),
            dma((mp - 1,)), dma((mp - 1,)),
        ],
        compiler_params=pltpu.CompilerParams(collective_id=1, has_side_effects=True),
        name="output",
    )(mixed, w_out, own, gain_part)


def stats_kernel(dp, mp, x_ref, all_ref, dp_send, dp_recv, mp_send, mp_recv, local_sem):
    d, m = lax.axis_index("dp"), lax.axis_index("mp")
    around = [(lax.rem(d + k, dp), m) for k in range(1, dp)]
    beside = [(d, lax.rem(m + k, mp)) for k in range(1, mp)]
    greet(around + beside)
    first = []
    for k in range(1, dp):
        copy = remote(
            x_ref, all_ref.at[m, d], dp_send.at[k - 1], dp_recv.at[k - 1], around[k - 1]
        )
        copy.start()
        first.append(copy)
    here = pltpu.make_async_copy(x_ref, all_ref.at[m, d], local_sem)
    here.start()
    here.wait()
    for copy in first:
        copy.wait()
    second = []
    for k in range(1, mp):
        copy = remote(
            all_ref.at[m], all_ref.at[m], mp_send.at[k - 1], mp_recv.at[k - 1], beside[k - 1]
        )
        copy.start()
        second.append(copy)
    for copy in second:
        copy.wait()


def gather_stats(stats, dp, mp):
    dma = pltpu.SemaphoreType.DMA
    return pl.pallas_call(
        functools.partial(stats_kernel, dp, mp),
        out_shape=jax.ShapeDtypeStruct((mp, dp) + stats.shape, stats.dtype),
        in_specs=[VMEM],
        out_specs=VMEM,
        scratch_shapes=[
            dma((dp - 1,)), dma((dp - 1,)), dma((mp - 1,)), dma((mp - 1,)), dma,
        ],
        compiler_params=pltpu.CompilerParams(collective_id=2, has_side_effects=True),
        name="stats",
    )(stats)


def local(
    embedded,
    targets,
    labels,
    counts,
    destinations,
    gain_in,
    w_query,
    w_key,
    w_value,
    w_out,
    gain_out,
    w_vocab,
    prev_probs,
    log_weights,
):
    dp = lax.axis_size("dp")
    mp = lax.axis_size("mp")
    data_index = lax.axis_index("dp")
    model_index = lax.axis_index("mp")
    chip = model_index // 2
    core = model_index % 2
    slots, seq_len, width = embedded.shape
    sequences = dp * slots // 2
    tokens = sequences * seq_len
    chips = mp // 2
    sibling = [(i, i ^ 1) for i in range(mp)]
    vocab_local = w_vocab.shape[1]
    columns = vocab_local // 2

    flat = embedded.reshape(slots * seq_len, width)
    given_columns = lax.dynamic_slice_in_dim(w_vocab, (1 - core) * columns, columns, 1)
    flat, given_columns = lax.optimization_barrier((flat, given_columns))
    taken_columns = lax.ppermute(given_columns, "mp", sibling)

    packed = jnp.concatenate([targets, labels[:, None], destinations[:, None]], axis=1)
    pad_rows, pad_columns = -slots % 8, -(seq_len + 2) % 128
    packed = jnp.pad(packed, ((0, pad_rows), (0, pad_columns)))
    full_rows, packed_all = gather_features(flat, packed, dp, mp)
    packed_all = packed_all[:, :slots].transpose(1, 0, 2).reshape(dp * slots, -1)
    is_live = (jnp.arange(slots)[:, None] < counts[None, :]).reshape(dp * slots)
    rank = jnp.cumsum(is_live.astype(jnp.int32)) - 1
    places = jnp.arange(sequences, dtype=jnp.int32)
    chosen = (rank[None, :] == places[:, None]) & is_live[None, :]
    entries = jnp.arange(dp * slots, dtype=jnp.int32)
    source = jnp.sum(jnp.where(chosen, entries[None, :], 0), axis=1).astype(jnp.int32)
    picked_ints = jnp.sum(jnp.where(chosen[:, :, None], packed_all[None], 0), axis=1)
    seq_targets = picked_ints[:, :seq_len]
    seq_labels = picked_ints[:, seq_len]
    seq_slots = picked_ints[:, seq_len + 1]

    mixed = attend(full_rows, gain_in, w_query, w_key, w_value, slots, seq_len)
    gain_part = lax.dynamic_slice_in_dim(gain_out, model_index * width, width, 0)
    final = project_output(mixed, w_out, flat, gain_part[None, :], mp)
    final = final.reshape(slots, seq_len, width)
    own_columns = lax.dynamic_slice_in_dim(w_vocab, core * columns, columns, 1)

    group = sequences // slots
    share = group // chips
    part = share * seq_len
    gathered = [
        lax.all_gather(final[j : j + 1], "dp", axis=0, tiled=True) for j in range(slots)
    ]

    def product(lhs, other):
        return jnp.dot(lhs, own_columns, preferred_element_type=jnp.float32) + jnp.dot(
            other, taken_columns, preferred_element_type=jnp.float32
        )

    ids = jnp.arange(columns, dtype=jnp.int32)
    tops, spreads, picks = [], [], []
    for j in range(slots):
        so_far = jnp.concatenate(gathered[: j + 1]) if j else gathered[0]
        order = jnp.roll(source[j * group : (j + 1) * group], -chip * share)
        rows = jnp.concatenate(
            [lax.dynamic_index_in_dim(so_far, order[i], 0, keepdims=True) for i in range(group)]
        ).reshape(group * seq_len, width)
        their_rows = lax.ppermute(rows, "mp", sibling)
        arrived = []
        for hop in range(1, chips):
            there = slice(hop * part, (hop + 1) * part)
            outgoing = product(rows[there], their_rows[there]).astype(jnp.bfloat16)
            across = [(i, (i + 2 * hop) % mp) for i in range(mp)]
            arrived.append(lax.ppermute(outgoing, "mp", across))
        logits = product(rows[:part], their_rows[:part])
        for piece in arrived:
            logits = logits + piece.astype(jnp.float32)
        goals = jnp.roll(seq_targets[j * group : (j + 1) * group], -chip * share, axis=0)
        goals = goals[:share].reshape(part) - (data_index * vocab_local + core * columns)
        top = jnp.max(logits, axis=1)
        tops.append(top)
        spreads.append(jnp.sum(jnp.exp(logits - top[:, None]), axis=1))
        picks.append(jnp.sum(jnp.where(ids[None, :] == goals[:, None], logits, 0.0), axis=1))
    stats = jnp.stack([jnp.concatenate(tops), jnp.concatenate(spreads), jnp.concatenate(picks)])
    stats = jnp.pad(stats, ((0, 5), (0, 0)))
    stats_all = gather_stats(stats, dp, mp).reshape(chips, 2 * dp, 8, slots * part)
    top_all = jnp.max(stats_all[:, :, 0], axis=1)
    scale = jnp.exp(stats_all[:, :, 0] - top_all[:, None])
    spread_all = jnp.sum(stats_all[:, :, 1] * scale, axis=1)
    picked_all = jnp.sum(stats_all[:, :, 2], axis=1)
    losses = top_all + jnp.log(spread_all) - picked_all
    losses = losses.reshape(chips, slots, part).transpose(1, 0, 2).reshape(sequences, seq_len)

    per_sequence = jnp.sum(losses, axis=1)
    domains = jnp.arange(DOMAINS, dtype=jnp.int32)
    member = (seq_labels[:, None] == domains[None, :]).astype(jnp.float32)
    loss_sums = jnp.sum(member * per_sequence[:, None], axis=0)
    token_tally = jnp.sum(member, axis=0) * seq_len
    placed = seq_slots[None, :] == places[:, None]
    losses = jnp.sum(jnp.where(placed[:, :, None], losses[None], 0.0), axis=1).reshape(tokens)
    block = tokens // (dp * mp)
    own_loss = lax.dynamic_slice_in_dim(
        losses, (data_index * mp + model_index) * block, block, 0
    )
    reward = loss_sums / jnp.maximum(token_tally, 1.0) / prev_probs
    new_weights = memory_rate * log_weights + (1.0 - memory_rate) * reward
    probs = (1.0 - DOMAINS * explore_mass) * jax.nn.softmax(step_rate * new_weights) + explore_mass
    return (own_loss, new_weights, probs)


def solution(mesh):
    placed = (
        P("dp", None, "mp"),
        P("dp", None),
        P("dp"),
        P(),
        P("dp"),
        P(),
        P(None, "mp"),
        P(None, "mp"),
        P(None, "mp"),
        P("mp", None),
        P(),
        P("mp", "dp"),
        P(),
        P(),
    )
    return jax.shard_map(
        local, mesh=mesh, in_specs=placed, out_specs=(P(("dp", "mp")), P(), P()), check_vma=False
    )
```

time: 358 us -> 396 us (1.11)
  blocking collectives: 75.1 us -> 0 us
  Pallas kernels: 0 us -> 58.2 us
  waiting for transfers between devices: 135 us -> 184 us
  matrix products: 54 us -> 62.1 us
  local copies, waits for them, and re-layouts: 28.4 us -> 20.6 us
  other arithmetic: 14.8 us -> 19.1 us
    all_gather x2 -> x4, waiting for transfers between devices: 32.9 us -> 125 us  [local(): lax.all_gather(final[j:j + 1], 'dp', axis=0, tiled=True)]
    all_gather x2 -> x0, blocking collectives: 69.3 us -> none  [the longest x1 42.3 us: local(): stats_all = lax.all_gather(stats, ('dp', 'mp'), axis=0, tiled=False)]
    pallas_call x0 -> x3, Pallas kernels: none -> 58.2 us  [the longest x1 23 us: gather_features(): pl.pallas_call(functools.partial(features_kernel, dp, mp), out_shape=(jax...]
    reduce_scatter x1 -> x0, waiting for transfers between devices: 30.5 us -> none  [local(): update = lax.psum_scatter(partial, 'mp', scatter_dimension=1, tiled=True)]
    ppermute x4, waiting for transfers between devices: 70.8 us -> 57.4 us  [local(): arrived.append(lax.ppermute(outgoing, 'mp', across))]
    unnamed x64 -> x40, local copies, waits for them, and re-layouts: 13.8 us -> 2.49 us
    dot_general x17 -> x16, matrix products: 45.6 us -> 53.6 us  [the longest x8 39.8 us: product(): jnp.dot(other, taken_columns, preferred_element_type=jnp.float32)]
    concatenate x1 -> x23, other arithmetic: 0.08 us -> 6.53 us  [the longest x3 3.34 us: local(): so_far = jnp.concatenate(gathered[:j + 1]) if j else gathered[0]]
  transfers between devices with their start and end apart: 9 -> 13, of which waited for: 7 -> 8; matrix products, arithmetic and copies ran while one was open for 17% -> 15% of each run, Pallas kernels for 0% -> 0%
where the time goes in v2:
time: 396 us; the launch traced here: 394 us
  waiting for transfers between devices  184 us (46%)
  matrix products  62.1 us (16%)
  Pallas kernels  58.2 us (15%)
  between operations  44.8 us (11%)
  local copies, waits for them, and re-layouts  20.6 us (5%)
  other arithmetic  19.1 us (5%)
  starting transfers between devices  5.23 us (1%)
    all_gather x4, waiting for transfers between devices, local(): lax.all_gather(final[j:j + 1], 'dp', axis=0, tiled=True)  125 us
    ppermute x4, waiting for transfers between devices, local(): arrived.append(lax.ppermute(outgoing, 'mp', across))  57.4 us
    dot_general x8, matrix products, product(): jnp.dot(other, taken_columns, preferred_element_type=jnp.float32)  39.8 us
    pallas_call x1, Pallas kernels, gather_features(): pl.pallas_call(functools.partial(features_kernel, dp, mp), out_shape=(jax...  23 us
    pallas_call x1, Pallas kernels, project_output(): pl.pallas_call(functools.partial(output_kernel, mp), out_shape=jax.ShapeD...  22.1 us
    dot_general x8, matrix products, product(): jnp.dot(lhs, own_columns, preferred_element_type=jnp.float32)  13.8 us
    pallas_call x1, Pallas kernels, gather_stats(): pl.pallas_call(functools.partial(stats_kernel, dp, mp), out_shape=jax.Sha...  13.2 us
  transfers between devices with their start and end apart: 13, of which 8 were waited for; matrix products, arithmetic and copies ran while one was open for 15% of the time, Pallas kernels for 0%

profile of v2, /device:TPU:0, one launch (start us, length us, event | category | flops | bytes accessed | tf_op | source)
XLA Modules:
  0.0 393.8 jit_solution(13971274377961408694)
XLA Ops:
  7.3 7.8 %constant_dynamic-slice_fusion.16 = bf16[1024,4096]{1,0:T(8,128)(2,1)} fusion(bf16[1024,8192]{1,0:T(8,128)(2,1)} %param.29, s32[]{:T(128)S(6)} %select_n.121), kind=kLoop, calls=%fused_computation.156 | loop fusion | bytes 16777220 | tf_op jit(solution)/shard_map/dynamic_slice | solution.py:354
  16.0 23.0 %features.1 = (bf16[256,4096]{1,0:T(8,128)(2,1)}, s32[8,8,128]{2,1,0:T(8,128)}) custom-call(bf16[256,1024]{1,0:T(8,128)(2,1)} %bitcast.124, s32[8,128]{1,0:T(8,128)} %pad.8.ints_ref), custom_call_target="tpu_custom_call" | custom-call | tf_op jit(solution)/shard_map/features/pallas_call | solution.py:155
  39.0 2.2 fusion.9
  41.3 3.5 fusion.90
  47.8 3.0 convolution_convert_fusion.1
  54.6 22.1 %output.1 = bf16[256,1024]{1,0:T(8,128)(2,1)} custom-call(bf16[256,512]{1,0:T(8,128)(2,1)} %reshape.286.mixed_ref, bf16[512,4096]{1,0:T(8,128)(2,1)} %w_ref.1, bf16[256,1024]{1,0:T(8,128)(2,1)} %bitcast.125, f32[1,1024]{1,0:T(1,128)} %bitcast.143), custom_call_target="tpu_custom_call" | custom-call | tf_op jit(solution)/shard_map/output/pallas_call | solution.py:257
  76.6 1.9 fusion.95
  116.6 41.1 %all-gather.13.cloned.1.call-done = bf16[512,1024]{1,0:T(8,128)(2,1)} async-done(((bf16[64,1024]{1,0:T(8,128)(2,1)}), bf16[512,1024]{1,0:T(8,128)(2,1)}) %all-gather.13.cloned.1.call-update) | async-done | bytes 1048592 | tf_op jit(solution)/shard_map/all_gather | solution.py:384
  157.8 41.2 %all-gather.11.cloned.1.call-done = bf16[512,1024]{1,0:T(8,128)(2,1)} async-done(((bf16[64,1024]{1,0:T(8,128)(2,1)}), bf16[512,1024]{1,0:T(8,128)(2,1)}) %all-gather.11.cloned.1.call-update) | async-done | bytes 1048592 | tf_op jit(solution)/shard_map/all_gather | solution.py:384
  198.9 41.0 %all-gather.9.cloned.1.call-done = bf16[512,1024]{1,0:T(8,128)(2,1)} async-done(((bf16[64,1024]{1,0:T(8,128)(2,1)}), bf16[512,1024]{1,0:T(8,128)(2,1)}) %all-gather.9.cloned.1.call-update) | async-done | bytes 1048592 | tf_op jit(solution)/shard_map/all_gather | solution.py:384
  239.9 2.6 pad_maximum_fusion
  247.6 4.8 %fusion.12 = f32[128,4096]{1,0:T(8,128)S(1)} fusion(bf16[128,1024]{1,0:T(8,128)(2,1)S(1)} %bitcast.126, bf16[1024,8192]{1,0:T(8,128)(2,1)} %param.29, s32[]{:T(128)S(6)} %select_n.129), kind=kOutput, calls=%fused_computation.44 | convolution fusion | flops 1073741824 | bytes 10747908 | tf_op jit(solution)/shard_map/dot_general | solution.py:388
  252.5 1.3 fusion.14
  253.8 1.3 fusion.16
  262.5 4.8 %fusion.8 = bf16[128,4096]{1,0:T(8,128)(2,1)S(1)} fusion(f32[128,4096]{1,0:T(8,128)S(1)} %fusion.12, bf16[1024,4096]{1,0:T(8,128)(2,1)} %collective-permute-done.1, bf16[256,1024]{1,0:T(8,128)(2,1)S(1)} %collective-permute-done.7), kind=kOutput, calls=%fused_computation.18 | convolution fusion | flops 1074790400 | bytes 11796480 | tf_op jit(solution)/shard_map/dot_general | solution.py:388
  267.3 1.5 collective-permute-start.8
  268.8 5.0 %fusion.7 = bf16[128,4096]{1,0:T(8,128)(2,1)S(1)} fusion(f32[128,4096]{1,0:T(8,128)S(1)} %fusion.16, bf16[1024,4096]{1,0:T(8,128)(2,1)} %collective-permute-done.1, bf16[256,1024]{1,0:T(8,128)(2,1)S(1)} %collective-permute-done.5), kind=kOutput, calls=%fused_computation.17 | convolution fusion | flops 1074790400 | bytes 11796480 | tf_op jit(solution)/shard_map/dot_general | solution.py:388
  274.5 4.8 %fusion.6 = bf16[128,4096]{1,0:T(8,128)(2,1)S(1)} fusion(f32[128,4096]{1,0:T(8,128)S(1)} %fusion.20, bf16[1024,4096]{1,0:T(8,128)(2,1)} %collective-permute-done.1, bf16[256,1024]{1,0:T(8,128)(2,1)S(1)} %collective-permute-done.3), kind=kOutput, calls=%fused_computation.16 | convolution fusion | flops 1074790400 | bytes 11796480 | tf_op jit(solution)/shard_map/dot_general | solution.py:388
  279.3 1.5 collective-permute-start.4
  280.8 4.8 %fusion.5 = bf16[128,4096]{1,0:T(8,128)(2,1)S(1)} fusion(f32[128,4096]{1,0:T(8,128)S(1)} %fusion.24, bf16[1024,4096]{1,0:T(8,128)(2,1)} %collective-permute-done.1, bf16[256,1024]{1,0:T(8,128)(2,1)S(1)} %collective-permute-done), kind=kOutput, calls=%fused_computation.15 | convolution fusion | flops 1074790400 | bytes 11796480 | tf_op jit(solution)/shard_map/dot_general | solution.py:388
  286.3 7.1 %collective-permute-done.8 = bf16[128,4096]{1,0:T(8,128)(2,1)S(1)} collective-permute-done((bf16[128,4096]{1,0:T(8,128)(2,1)S(1)}, bf16[128,4096]{1,0:T(8,128)(2,1)S(1)}, u32[]{:S(2)}, u32[]{:S(2)}) %collective-permute-start.8) | collective-permute-done | bytes 1048608 | tf_op jit(solution)/shard_map/ppermute | solution.py:406
  293.4 5.1 %fusion.106 = (f32[128]{0:T(128)S(1)}, f32[128,4096]{1,0:T(8,128)S(1)}) fusion(bf16[128,4096]{1,0:T(8,128)(2,1)S(1)} %collective-permute-done.8, f32[128,4096]{1,0:T(8,128)S(1)} %fusion.14, bf16[1024,4096]{1,0:T(8,128)(2,1)} %collective-permute-done.1, bf16[256,1024]{1,0:T(8,128)(2,1)S(1)} %collective-permute-done.7), kind=kOutput, calls=%fused_computation.204 | convolution fusion | flops 1075838848 | bytes 13894144 | tf_op jit(solution)/shard_map/dot_general | solution.py:388
  298.5 17.3 %collective-permute-done.6 = bf16[128,4096]{1,0:T(8,128)(2,1)S(1)} collective-permute-done((bf16[128,4096]{1,0:T(8,128)(2,1)S(1)}, bf16[128,4096]{1,0:T(8,128)(2,1)S(1)}, u32[]{:S(2)}, u32[]{:S(2)}) %collective-permute-start.6) | collective-permute-done | bytes 1048608 | tf_op jit(solution)/shard_map/ppermute | solution.py:406
  315.9 5.1 %fusion.107 = (f32[128]{0:T(128)S(1)}, f32[128,4096]{1,0:T(8,128)S(1)}) fusion(bf16[128,4096]{1,0:T(8,128)(2,1)S(1)} %collective-permute-done.6, f32[128,4096]{1,0:T(8,128)S(1)} %fusion.18, bf16[1024,4096]{1,0:T(8,128)(2,1)} %collective-permute-done.1, bf16[256,1024]{1,0:T(8,128)(2,1)S(1)} %collective-permute-done.5), kind=kOutput, calls=%fused_computation.205 | convolution fusion | flops 1075838848 | bytes 13894144 | tf_op jit(solution)/shard_map/dot_general | solution.py:388
  322.4 15.9 %collective-permute-done.4 = bf16[128,4096]{1,0:T(8,128)(2,1)S(1)} collective-permute-done((bf16[128,4096]{1,0:T(8,128)(2,1)S(1)}, bf16[128,4096]{1,0:T(8,128)(2,1)S(1)}, u32[]{:S(2)}, u32[]{:S(2)}) %collective-permute-start.4) | collective-permute-done | bytes 1048608 | tf_op jit(solution)/shard_map/ppermute | solution.py:406
  338.3 5.1 %fusion.108 = (f32[128]{0:T(128)S(1)}, f32[128,4096]{1,0:T(8,128)S(1)}) fusion(bf16[128,4096]{1,0:T(8,128)(2,1)S(1)} %collective-permute-done.4, f32[128,4096]{1,0:T(8,128)S(1)} %fusion.22, bf16[1024,4096]{1,0:T(8,128)(2,1)} %collective-permute-done.1, bf16[256,1024]{1,0:T(8,128)(2,1)S(1)} %collective-permute-done.3), kind=kOutput, calls=%fused_computation.206 | convolution fusion | flops 1075838848 | bytes 13894144 | tf_op jit(solution)/shard_map/dot_general | solution.py:388
  343.4 17.0 %collective-permute-done.2 = bf16[128,4096]{1,0:T(8,128)(2,1)S(1)} collective-permute-done((bf16[128,4096]{1,0:T(8,128)(2,1)S(1)}, bf16[128,4096]{1,0:T(8,128)(2,1)S(1)}, u32[]{:S(2)}, u32[]{:S(2)}) %collective-permute-start.2) | collective-permute-done | bytes 1048608 | tf_op jit(solution)/shard_map/ppermute | solution.py:406
  360.4 5.1 %fusion.109 = (f32[128]{0:T(128)S(1)}, f32[128,4096]{1,0:T(8,128)S(1)}) fusion(bf16[128,4096]{1,0:T(8,128)(2,1)S(1)} %collective-permute-done.2, f32[128,4096]{1,0:T(8,128)S(1)} %fusion.26, bf16[1024,4096]{1,0:T(8,128)(2,1)} %collective-permute-done.1, bf16[256,1024]{1,0:T(8,128)(2,1)S(1)} %collective-permute-done), kind=kOutput, calls=%fused_computation.207 | convolution fusion | flops 1075838848 | bytes 13894144 | tf_op jit(solution)/shard_map/dot_general | solution.py:388
  367.5 13.2 %stats.1 = f32[4,8,8,512]{3,2,1,0:T(8,128)} custom-call(f32[8,512]{1,0:T(8,128)} %select_maximum_fusion.x_ref), custom_call_target="tpu_custom_call" | custom-call | tf_op jit(solution)/shard_map/stats/pallas_call | solution.py:310
  380.7 1.6 slice_reduce_fusion.3
  383.4 1.3 fusion.88
  384.8 1.9 multiply_add_fusion
  (160 shorter events, 34.0 us)
Async XLA Ops:
  7.2 38.5 %copy-start = (bf16[4096,256]{1,0:T(8,128)(2,1)S(1)}, bf16[4096,256]{1,0:T(8,128)(2,1)}, u32[]{:S(2)}) copy-start(bf16[4096,256]{1,0:T(8,128)(2,1)} %param.25) | copy-start | bytes 6291460
  7.2 109.4 %all-gather.15.cloned.1.call-start = ((), (), s32[]{:S(2)}) async-start(), calls=%async_computation.3 | async-start | bytes 1179648 | tf_op jit(solution)/shard_map/all_gather | solution.py:384
  7.3 7.9 %copy-start.10 = (s32[4]{0:T(128)S(1)}, s32[4]{0:T(128)}, u32[]{:S(2)}) copy-start(s32[4]{0:T(128)} %param.22) | copy-start | bytes 52
  7.3 8.0 %copy-start.11 = (s32[4]{0:T(128)S(1)}, s32[4]{0:T(128)}, u32[]{:S(2)}) copy-start(s32[4]{0:T(128)} %param.20) | copy-start | bytes 52
  7.3 8.0 %copy-start.8 = (s32[4,64]{1,0:T(4,128)S(1)}, s32[4,64]{1,0:T(4,128)}, u32[]{:S(2)}) copy-start(s32[4,64]{1,0:T(4,128)} %param.19) | copy-start | bytes 3076
  15.2 26.1 %copy-start.15 = (f32[4096]{0:T(1024)S(1)}, f32[4096]{0:T(1024)}, u32[]{:S(2)}) copy-start(f32[4096]{0:T(1024)} %param.23) | copy-start | bytes 49156
  39.0 2.3 copy-start.5
  45.0 1.6 copy-start.6
  54.5 26.1 %copy-start.12 = (s32[8]{0:T(128)S(1)}, s32[8]{0:T(128)}, u32[]{:S(2)}) copy-start(s32[8]{0:T(128)} %param.21) | copy-start | bytes 100
  54.5 26.5 %copy-start.7 = (s32[8,8,128]{2,1,0:T(8,128)S(1)}, s32[8,8,128]{2,1,0:T(8,128)}, u32[]{:S(2)}) copy-start(s32[8,8,128]{2,1,0:T(8,128)} %get-tuple-element.10) | copy-start | bytes 98308
  78.6 79.2 %all-gather.13.cloned.1.call-start = ((), (), s32[]{:S(2)}) async-start(), calls=%async_computation.2 | async-start | bytes 1179648 | tf_op jit(solution)/shard_map/all_gather | solution.py:384
  79.3 119.6 %all-gather.11.cloned.1.call-start = ((), (), s32[]{:S(2)}) async-start(), calls=%async_computation.1 | async-start | bytes 1179648 | tf_op jit(solution)/shard_map/all_gather | solution.py:384
  80.0 159.9 %all-gather.9.cloned.1.call-start = ((), (), s32[]{:S(2)}) async-start(), calls=%async_computation | async-start | bytes 1179648 | tf_op jit(solution)/shard_map/all_gather | solution.py:384
  80.1 182.4 %collective-permute-start.1 = (bf16[1024,4096]{1,0:T(8,128)(2,1)}, bf16[1024,4096]{1,0:T(8,128)(2,1)}, u32[]{:S(2)}, u32[]{:S(2)}) collective-permute-start(bf16[1024,4096]{1,0:T(8,128)(2,1)} %constant_dynamic-slice_fusion.16), channel_id=1, source_target_pairs={{0,1},{1,0},{2,3},{3,2},{4,5},{5,4},{6,7},{7,6},{8,9},{9,8},{10,11... | collective-permute-start | bytes 25165832 | tf_op jit(solution)/shard_map/ppermute | solution.py:356
  239.9 2.8 copy-start.4
  239.9 12.5 %slice-start = ((s8[16777216]{0:T(1024)(128)(4,1)}), s8[4194304]{0:T(1024)(128)(4,1)S(1)}, s32[]{:S(2)}) async-start(s8[16777216]{0:T(1024)(128)(4,1)} %bitcast.114), calls=%async_computation.4 | async-start | bytes 8388608
  242.5 1.8 copy-start.3
  242.6 9.9 %slice-start.1 = ((s8[16777216]{0:T(1024)(128)(4,1)}), s8[4194304]{0:T(1024)(128)(4,1)S(1)}, s32[]{:S(2)}) async-start(s8[16777216]{0:T(1024)(128)(4,1)} %bitcast.114), calls=%async_computation.5 | async-start | bytes 8388608
  242.7 19.8 %collective-permute-start.7 = (bf16[256,1024]{1,0:T(8,128)(2,1)S(1)}, bf16[256,1024]{1,0:T(8,128)(2,1)S(1)}, u32[]{:S(2)}, u32[]{:S(2)}) collective-permute-start(bf16[256,1024]{1,0:T(8,128)(2,1)S(1)} %bitcast.136), channel_id=1, source_target_pairs={{0,1},{1,0},{2,3},{3,2},{4,5},{5,4},{6,7},{7,6},{8,9},{9,8},{10,11... | collective-permute-start | bytes 1572872 | tf_op jit(solution)/shard_map/ppermute | solution.py:400
  245.7 6.7 %slice-start.2 = ((s8[16777216]{0:T(1024)(128)(4,1)}), s8[4194304]{0:T(1024)(128)(4,1)S(1)}, s32[]{:S(2)}) async-start(s8[16777216]{0:T(1024)(128)(4,1)} %bitcast.114), calls=%async_computation.6 | async-start | bytes 8388608
  245.8 23.1 %collective-permute-start.5 = (bf16[256,1024]{1,0:T(8,128)(2,1)}, bf16[256,1024]{1,0:T(8,128)(2,1)S(1)}, u32[]{:S(2)}, u32[]{:S(2)}) collective-permute-start(bf16[256,1024]{1,0:T(8,128)(2,1)} %bitcast.35), channel_id=1, source_target_pairs={{0,1},{1,0},{2,3},{3,2},{4,5},{5,4},{6,7},{7,6},{8,9},{9,8},{10,11... | collective-permute-start | bytes 1572872 | tf_op jit(solution)/shard_map/ppermute | solution.py:400
  246.8 27.7 %collective-permute-start.3 = (bf16[256,1024]{1,0:T(8,128)(2,1)}, bf16[256,1024]{1,0:T(8,128)(2,1)S(1)}, u32[]{:S(2)}, u32[]{:S(2)}) collective-permute-start(bf16[256,1024]{1,0:T(8,128)(2,1)} %bitcast.27), channel_id=1, source_target_pairs={{0,1},{1,0},{2,3},{3,2},{4,5},{5,4},{6,7},{7,6},{8,9},{9,8},{10,11... | collective-permute-start | bytes 1572872 | tf_op jit(solution)/shard_map/ppermute | solution.py:400
  247.6 4.9 %slice-start.3 = ((s8[16777216]{0:T(1024)(128)(4,1)}), s8[4194304]{0:T(1024)(128)(4,1)S(1)}, s32[]{:S(2)}) async-start(s8[16777216]{0:T(1024)(128)(4,1)} %bitcast.114), calls=%async_computation.7 | async-start | bytes 8388608
  261.2 19.7 %collective-permute-start = (bf16[256,1024]{1,0:T(8,128)(2,1)}, bf16[256,1024]{1,0:T(8,128)(2,1)S(1)}, u32[]{:S(2)}, u32[]{:S(2)}) collective-permute-start(bf16[256,1024]{1,0:T(8,128)(2,1)} %bitcast.19), channel_id=1, source_target_pairs={{0,1},{1,0},{2,3},{3,2},{4,5},{5,4},{6,7},{7,6},{8,9},{9,8},{10,11... | collective-permute-start | bytes 1572872 | tf_op jit(solution)/shard_map/ppermute | solution.py:400
  267.3 26.1 %collective-permute-start.8 = (bf16[128,4096]{1,0:T(8,128)(2,1)S(1)}, bf16[128,4096]{1,0:T(8,128)(2,1)S(1)}, u32[]{:S(2)}, u32[]{:S(2)}) collective-permute-start(bf16[128,4096]{1,0:T(8,128)(2,1)S(1)} %fusion.8), channel_id=1, source_target_pairs={{0,2},{1,3},{2,0},{3,1},{4,6},{5,7},{6,4},{7,5},{8,10},{9,11},{10,... | collective-permute-start | bytes 3145736 | tf_op jit(solution)/shard_map/ppermute | solution.py:406
  273.9 42.0 %collective-permute-start.6 = (bf16[128,4096]{1,0:T(8,128)(2,1)S(1)}, bf16[128,4096]{1,0:T(8,128)(2,1)S(1)}, u32[]{:S(2)}, u32[]{:S(2)}) collective-permute-start(bf16[128,4096]{1,0:T(8,128)(2,1)S(1)} %fusion.7), channel_id=1, source_target_pairs={{0,2},{1,3},{2,0},{3,1},{4,6},{5,7},{6,4},{7,5},{8,10},{9,11},{10,... | collective-permute-start | bytes 3145736 | tf_op jit(solution)/shard_map/ppermute | solution.py:406
  279.3 59.0 %collective-permute-start.4 = (bf16[128,4096]{1,0:T(8,128)(2,1)S(1)}, bf16[128,4096]{1,0:T(8,128)(2,1)S(1)}, u32[]{:S(2)}, u32[]{:S(2)}) collective-permute-start(bf16[128,4096]{1,0:T(8,128)(2,1)S(1)} %fusion.6), channel_id=1, source_target_pairs={{0,2},{1,3},{2,0},{3,1},{4,6},{5,7},{6,4},{7,5},{8,10},{9,11},{10,... | collective-permute-start | bytes 3145736 | tf_op jit(solution)/shard_map/ppermute | solution.py:406
  285.6 74.7 %collective-permute-start.2 = (bf16[128,4096]{1,0:T(8,128)(2,1)S(1)}, bf16[128,4096]{1,0:T(8,128)(2,1)S(1)}, u32[]{:S(2)}, u32[]{:S(2)}) collective-permute-start(bf16[128,4096]{1,0:T(8,128)(2,1)S(1)} %fusion.5), channel_id=1, source_target_pairs={{0,2},{1,3},{2,0},{3,1},{4,6},{5,7},{6,4},{7,5},{8,10},{9,11},{10,... | collective-permute-start | bytes 3145736 | tf_op jit(solution)/shard_map/ppermute | solution.py:406
  365.4 21.8 %copy-start.1 = (bf16[4096,256]{1,0:T(8,128)(2,1)S(1)}, bf16[4096,256]{1,0:T(8,128)(2,1)}, u32[]{:S(2)}) copy-start(bf16[4096,256]{1,0:T(8,128)(2,1)} %param.25) | copy-start | bytes 6291460
  366.2 16.7 %copy-start.13 = (f32[22]{0:T(128)S(1)}, f32[22]{0:T(128)}, u32[]{:S(2)}) copy-start(f32[22]{0:T(128)} %param.30) | copy-start | bytes 268
  366.2 16.7 %copy-start.14 = (f32[22]{0:T(128)S(1)}, f32[22]{0:T(128)}, u32[]{:S(2)}) copy-start(f32[22]{0:T(128)} %param.31) | copy-start | bytes 268
  383.4 3.8 copy-start.9
  (1 other events, 1.5 us)
Sparse Core Ops, SparseCore 0:
  78.7 37.8 all-gather.14
  118.7 38.9 all-gather.12
  159.9 38.9 all-gather.10
  200.9 38.9 all-gather.8

commit v3 on v2

--- a/solution.py
+++ b/solution.py
@@ -10,6 +10,7 @@
 HEAD_DIM = 128
 DOMAINS = 22
 PIECES = 4
+CHUNKS = 4
 MESH = pl.DeviceIdType.MESH
 VMEM = pl.BlockSpec(memory_space=pltpu.VMEM)
 
@@ -320,6 +321,88 @@
     )(stats)
 
 
+def rows_kernel(
+    dp, order_ref, x_ref, rows_ref, all_ref, mate_send, mate_recv, line_send, line_recv, local_sem
+):
+    d, m = lax.axis_index("dp"), lax.axis_index("mp")
+    slots = x_ref.shape[0]
+    length = dp // 2
+    where, side = d // 2, d % 2
+    mate = where * 2 + (1 - side)
+    after = [lax.rem(where + k, length) for k in range(length)]
+    before = [lax.rem(where + length - k, length) for k in range(length)]
+    line = [(after[k] * 2 + side, m) for k in range(1, length)]
+    greet([(mate, m)] + line)
+
+    def place(block, slot):
+        return all_ref.at[block * slots + slot]
+
+    def to_mate(src, block, k, slot):
+        copy = remote(
+            src, place(block, slot), mate_send.at[k, slot], mate_recv.at[k, slot], (mate, m)
+        )
+        copy.start()
+        return copy
+
+    def to_line(src, block, k, turn, slot):
+        copy = remote(
+            src, place(block, slot), line_send.at[turn, k - 1, slot],
+            line_recv.at[turn, k - 1, slot], line[k - 1],
+        )
+        copy.start()
+        return copy
+
+    mates, lines = {}, {}
+    here = pltpu.make_async_copy(x_ref, all_ref.at[pl.ds(d * slots, slots)], local_sem)
+    here.start()
+    for slot in range(slots):
+        mates[0, slot] = to_mate(x_ref.at[slot], d, 0, slot)
+        for k in range(1, length):
+            lines[0, k, slot] = to_line(x_ref.at[slot], d, k, 0, slot)
+    for slot in range(slots):
+        if slot % 2:
+            mates[0, slot].wait_recv()
+            for k in range(1, length):
+                lines[1, k, slot] = to_line(place(mate, slot), mate, k, 1, slot)
+        else:
+            for k in range(1, length):
+                lines[0, k, slot].wait_recv()
+                block = before[k] * 2 + side
+                mates[k, slot] = to_mate(place(block, slot), block, k, slot)
+    here.wait()
+    for (k, slot), copy in mates.items():
+        if slot % 2 and k == 0:
+            copy.wait_send()
+        else:
+            copy.wait()
+    for (turn, k, slot), copy in lines.items():
+        if slot % 2 == 0 and turn == 0:
+            copy.wait_send()
+        else:
+            copy.wait()
+    for i in range(rows_ref.shape[0]):
+        rows_ref[i] = all_ref[order_ref[i]]
+
+
+def gather_rows(order, final, dp):
+    slots, seq_len, width = final.shape
+    dma = pltpu.SemaphoreType.DMA
+    length = dp // 2
+    return pl.pallas_call(
+        functools.partial(rows_kernel, dp),
+        out_shape=jax.ShapeDtypeStruct((order.shape[0], seq_len, width), final.dtype),
+        in_specs=[pl.BlockSpec(memory_space=pltpu.SMEM), VMEM],
+        out_specs=VMEM,
+        scratch_shapes=[
+            pltpu.VMEM((dp * slots, seq_len, width), final.dtype),
+            dma((length, slots)), dma((length, slots)),
+            dma((2, length - 1, slots)), dma((2, length - 1, slots)), dma,
+        ],
+        compiler_params=pltpu.CompilerParams(collective_id=3, has_side_effects=True),
+        name="rows",
+    )(order, final)
+
+
 def local(
     embedded,
     targets,
@@ -352,84 +435,79 @@
 
     flat = embedded.reshape(slots * seq_len, width)
     given_columns = lax.dynamic_slice_in_dim(w_vocab, (1 - core) * columns, columns, 1)
-    flat, given_columns = lax.optimization_barrier((flat, given_columns))
     taken_columns = lax.ppermute(given_columns, "mp", sibling)
+    own_columns = lax.dynamic_slice_in_dim(w_vocab, core * columns, columns, 1)
 
     packed = jnp.concatenate([targets, labels[:, None], destinations[:, None]], axis=1)
     pad_rows, pad_columns = -slots % 8, -(seq_len + 2) % 128
     packed = jnp.pad(packed, ((0, pad_rows), (0, pad_columns)))
     full_rows, packed_all = gather_features(flat, packed, dp, mp)
-    packed_all = packed_all[:, :slots].transpose(1, 0, 2).reshape(dp * slots, -1)
-    is_live = (jnp.arange(slots)[:, None] < counts[None, :]).reshape(dp * slots)
-    rank = jnp.cumsum(is_live.astype(jnp.int32)) - 1
+    packed_all = packed_all[:, :slots].reshape(dp * slots, -1)
+    entries = jnp.arange(dp * slots, dtype=jnp.int32)
+    is_live = entries % slots < counts[entries // slots]
     places = jnp.arange(sequences, dtype=jnp.int32)
-    chosen = (rank[None, :] == places[:, None]) & is_live[None, :]
-    entries = jnp.arange(dp * slots, dtype=jnp.int32)
+    chosen = (packed_all[:, seq_len + 1][None, :] == places[:, None]) & is_live[None, :]
     source = jnp.sum(jnp.where(chosen, entries[None, :], 0), axis=1).astype(jnp.int32)
     picked_ints = jnp.sum(jnp.where(chosen[:, :, None], packed_all[None], 0), axis=1)
     seq_targets = picked_ints[:, :seq_len]
     seq_labels = picked_ints[:, seq_len]
-    seq_slots = picked_ints[:, seq_len + 1]
+    seq_part = sequences // chips
+    order = jnp.roll(source, -chip * seq_part)
 
     mixed = attend(full_rows, gain_in, w_query, w_key, w_value, slots, seq_len)
     gain_part = lax.dynamic_slice_in_dim(gain_out, model_index * width, width, 0)
     final = project_output(mixed, w_out, flat, gain_part[None, :], mp)
     final = final.reshape(slots, seq_len, width)
-    own_columns = lax.dynamic_slice_in_dim(w_vocab, core * columns, columns, 1)
-
-    group = sequences // slots
-    share = group // chips
-    part = share * seq_len
-    gathered = [
-        lax.all_gather(final[j : j + 1], "dp", axis=0, tiled=True) for j in range(slots)
-    ]
-
-    def product(lhs, other):
-        return jnp.dot(lhs, own_columns, preferred_element_type=jnp.float32) + jnp.dot(
-            other, taken_columns, preferred_element_type=jnp.float32
-        )
-
-    ids = jnp.arange(columns, dtype=jnp.int32)
-    tops, spreads, picks = [], [], []
-    for j in range(slots):
-        so_far = jnp.concatenate(gathered[: j + 1]) if j else gathered[0]
-        order = jnp.roll(source[j * group : (j + 1) * group], -chip * share)
-        rows = jnp.concatenate(
-            [lax.dynamic_index_in_dim(so_far, order[i], 0, keepdims=True) for i in range(group)]
-        ).reshape(group * seq_len, width)
-        their_rows = lax.ppermute(rows, "mp", sibling)
-        arrived = []
+    rows = gather_rows(order, final, dp).reshape(tokens, width)
+    their_rows = lax.ppermute(rows, "mp", sibling)
+    part = tokens // chips
+    goals = jnp.roll(seq_targets, -chip * seq_part, axis=0)[:seq_part].reshape(part)
+    goals = goals - (data_index * vocab_local + core * columns)
+
+    def product(lhs, other, start, size):
+        return jnp.dot(
+            lhs, own_columns[:, start : start + size], preferred_element_type=jnp.float32
+        ) + jnp.dot(
+            other, taken_columns[:, start : start + size], preferred_element_type=jnp.float32
+        )
+
+    size = columns // CHUNKS
+    arrived = []
+    for i in range(CHUNKS):
+        hops = []
         for hop in range(1, chips):
             there = slice(hop * part, (hop + 1) * part)
-            outgoing = product(rows[there], their_rows[there]).astype(jnp.bfloat16)
-            across = [(i, (i + 2 * hop) % mp) for i in range(mp)]
-            arrived.append(lax.ppermute(outgoing, "mp", across))
-        logits = product(rows[:part], their_rows[:part])
-        for piece in arrived:
+            outgoing = product(rows[there], their_rows[there], i * size, size)
+            across = [(j, (j + 2 * hop) % mp) for j in range(mp)]
+            hops.append(lax.ppermute(outgoing.astype(jnp.bfloat16), "mp", across))
+        arrived.append(hops)
+    tops, spreads, picks = [], [], []
+    for i in range(CHUNKS):
+        logits = product(rows[:part], their_rows[:part], i * size, size)
+        for piece in arrived[i]:
             logits = logits + piece.astype(jnp.float32)
-        goals = jnp.roll(seq_targets[j * group : (j + 1) * group], -chip * share, axis=0)
-        goals = goals[:share].reshape(part) - (data_index * vocab_local + core * columns)
         top = jnp.max(logits, axis=1)
         tops.append(top)
         spreads.append(jnp.sum(jnp.exp(logits - top[:, None]), axis=1))
+        ids = i * size + jnp.arange(size, dtype=jnp.int32)
         picks.append(jnp.sum(jnp.where(ids[None, :] == goals[:, None], logits, 0.0), axis=1))
-    stats = jnp.stack([jnp.concatenate(tops), jnp.concatenate(spreads), jnp.concatenate(picks)])
-    stats = jnp.pad(stats, ((0, 5), (0, 0)))
-    stats_all = gather_stats(stats, dp, mp).reshape(chips, 2 * dp, 8, slots * part)
+    top = functools.reduce(jnp.maximum, tops)
+    spread = sum(own * jnp.exp(high - top) for own, high in zip(spreads, tops))
+    stats = jnp.pad(jnp.stack([top, spread, sum(picks)]), ((0, 5), (0, 0)))
+    stats_all = gather_stats(stats, dp, mp).reshape(chips, 2 * dp, 8, part)
     top_all = jnp.max(stats_all[:, :, 0], axis=1)
     scale = jnp.exp(stats_all[:, :, 0] - top_all[:, None])
     spread_all = jnp.sum(stats_all[:, :, 1] * scale, axis=1)
     picked_all = jnp.sum(stats_all[:, :, 2], axis=1)
-    losses = top_all + jnp.log(spread_all) - picked_all
-    losses = losses.reshape(chips, slots, part).transpose(1, 0, 2).reshape(sequences, seq_len)
+    losses = (top_all + jnp.log(spread_all) - picked_all).reshape(sequences, seq_len)
 
     per_sequence = jnp.sum(losses, axis=1)
     domains = jnp.arange(DOMAINS, dtype=jnp.int32)
     member = (seq_labels[:, None] == domains[None, :]).astype(jnp.float32)
     loss_sums = jnp.sum(member * per_sequence[:, None], axis=0)
     token_tally = jnp.sum(member, axis=0) * seq_len
-    placed = seq_slots[None, :] == places[:, None]
-    losses = jnp.sum(jnp.where(placed[:, :, None], losses[None], 0.0), axis=1).reshape(tokens)
+    losses = losses.reshape(tokens)
+
     block = tokens // (dp * mp)
     own_loss = lax.dynamic_slice_in_dim(
         losses, (data_index * mp + model_index) * block, block, 0

time: 396 us -> 290 us (0.73)
  waiting for transfers between devices: 184 us -> 68.9 us
  Pallas kernels: 58.2 us -> 132 us
  between operations: 44.8 us -> 1.16 us
  matrix products: 62.1 us -> 51.8 us
  other arithmetic: 19.1 us -> 12.5 us
    all_gather x4 -> x0, waiting for transfers between devices: 125 us -> none  [local(): lax.all_gather(final[j:j + 1], 'dp', axis=0, tiled=True)]
    pallas_call x0 -> x1, Pallas kernels: none -> 72.6 us  [gather_rows(): pl.pallas_call(functools.partial(rows_kernel, dp), out_shape=jax.ShapeDty...]
    ppermute x4, waiting for transfers between devices: 57.4 us -> 68.9 us  [local(): hops.append(lax.ppermute(outgoing.astype(jnp.bfloat16), 'mp', across))]
    dot_general x16, matrix products: 53.6 us -> 43.3 us  [the longest x8 26.3 us: product(): jnp.dot(other, taken_columns[:, start:start + size], preferred_element_ty...]
    concatenate x22 -> x1, other arithmetic: 6.46 us -> 0.08 us  [local(): order = jnp.roll(source, -chip * seq_part)]
  transfers between devices with their start and end apart: 13 -> 6, of which waited for: 8 -> 4; matrix products, arithmetic and copies ran while one was open for 15% -> 20% of each run, Pallas kernels for 0% -> 41%
where the time goes in v3:
time: 290 us; the launch traced here: 289 us
  Pallas kernels  132 us (46%)
  waiting for transfers between devices  68.9 us (24%)
  matrix products  51.8 us (18%)
  local copies, waits for them, and re-layouts  17.7 us (6%)
  other arithmetic  12.5 us (4%)
  starting transfers between devices  4.88 us (2%)
    pallas_call x1, Pallas kernels, gather_rows(): pl.pallas_call(functools.partial(rows_kernel, dp), out_shape=jax.ShapeDty...  72.6 us
    ppermute x4, waiting for transfers between devices, local(): hops.append(lax.ppermute(outgoing.astype(jnp.bfloat16), 'mp', across))  68.9 us
    dot_general x8, matrix products, product(): jnp.dot(other, taken_columns[:, start:start + size], preferred_element_ty...  26.3 us
    pallas_call x1, Pallas kernels, gather_features(): pl.pallas_call(functools.partial(features_kernel, dp, mp), out_shape=(jax...  23.1 us
    pallas_call x1, Pallas kernels, project_output(): pl.pallas_call(functools.partial(output_kernel, mp), out_shape=jax.ShapeD...  22 us
    dot_general x8, matrix products, product(): jnp.dot(lhs, own_columns[:, start:start + size], preferred_element_type=j...  17 us
    pallas_call x1, Pallas kernels, gather_stats(): pl.pallas_call(functools.partial(stats_kernel, dp, mp), out_shape=jax.Sha...  14.2 us
    dynamic_slice x1, local copies, waits for them, and re-layouts, local(): lax.dynamic_slice_in_dim(w_vocab, (1 - core) * columns, columns, 1)  7.85 us
  transfers between devices with their start and end apart: 6, of which 4 were waited for; matrix products, arithmetic and copies ran while one was open for 20% of the time, Pallas kernels for 41%

profile of v3, /device:TPU:0, one launch (start us, length us, event | category | flops | bytes accessed | tf_op | source)
XLA Modules:
  0.0 288.9 jit_solution(6818997997893873861)
XLA Ops:
  0.7 7.9 %constant_dynamic-slice_fusion = bf16[1024,4096]{1,0:T(8,128)(2,1)} fusion(bf16[1024,8192]{1,0:T(8,128)(2,1)} %param.25, s32[]{:T(128)S(6)} %select_n.109), kind=kLoop, calls=%fused_computation.129 | loop fusion | bytes 16777220 | tf_op jit(solution)/shard_map/dynamic_slice | solution.py:437
  9.9 23.1 %features.1 = (bf16[256,4096]{1,0:T(8,128)(2,1)}, s32[8,8,128]{2,1,0:T(8,128)}) custom-call(bf16[256,1024]{1,0:T(8,128)(2,1)} %bitcast.85, s32[8,128]{1,0:T(8,128)} %pad.8.ints_ref), custom_call_target="tpu_custom_call" | custom-call | tf_op jit(solution)/shard_map/features/pallas_call | solution.py:156
  33.9 2.2 fusion.1
  37.2 4.1 %fusion.113 = f32[256,512]{1,0:T(8,128)S(1)} fusion(bf16[4096,512]{1,0:T(8,128)(2,1)} %param.20, bf16[256,4096]{1,0:T(8,128)(2,1)} %get-tuple-element.6, f32[4096]{0:T(1024)S(1)} %copy-done.11, f32[256]{0:T(256)S(1)} %add_rsqrt_fusion), kind=kOutput, calls=%fused_computation.154 | convolution fusion | flops 1077936128 | bytes 6833152 | tf_op jit(solution)/shard_map/dot_general | solution.py:48
  43.1 2.4 convolution_convert_fusion.1
  51.1 22.0 %output.1 = bf16[256,1024]{1,0:T(8,128)(2,1)} custom-call(bf16[256,512]{1,0:T(8,128)(2,1)} %reshape.362.mixed_ref, bf16[512,4096]{1,0:T(8,128)(2,1)} %w_ref.1, bf16[256,1024]{1,0:T(8,128)(2,1)} %bitcast.86, f32[1,1024]{1,0:T(1,128)} %bitcast.106), custom_call_target="tpu_custom_call" | custom-call | tf_op jit(solution)/shard_map/output/pallas_call | solution.py:258
  73.1 72.6 %rows.1 = bf16[16,64,1024]{2,1,0:T(8,128)(2,1)} custom-call(s32[16]{0:T(128)} %dynamic_slice.20.order_ref, bf16[4,64,1024]{2,1,0:T(8,128)(2,1)} %bitcast.87), custom_call_target="tpu_custom_call" | custom-call | tf_op jit(solution)/shard_map/rows/pallas_call | solution.py:391
  146.1 1.9 fusion.118
  148.0 3.0 %fusion.32 = f32[512,1024]{1,0:T(8,128)S(1)} fusion(bf16[512,1024]{1,0:T(8,128)(2,1)S(1)} %bitcast.92, bf16[1024,8192]{1,0:T(8,128)(2,1)} %param.25, s32[]{:T(128)S(6)} %select_n.108), kind=kOutput, calls=%fused_computation.52 | convolution fusion | flops 1073741824 | bytes 5242884 | tf_op jit(solution)/shard_map/dot_general | solution.py:468
  151.0 3.0 %fusion.34 = f32[512,1024]{1,0:T(8,128)S(1)} fusion(bf16[512,1024]{1,0:T(8,128)(2,1)S(1)} %bitcast.88, bf16[1024,8192]{1,0:T(8,128)(2,1)} %param.25, s32[]{:T(128)S(6)} %select_n.108), kind=kOutput, calls=%fused_computation.54 | convolution fusion | flops 1073741824 | bytes 5242884 | tf_op jit(solution)/shard_map/dot_general | solution.py:468
  154.2 3.0 %fusion.20 = f32[512,1024]{1,0:T(8,128)S(1)} fusion(bf16[512,1024]{1,0:T(8,128)(2,1)S(1)} %bitcast.93, bf16[1024,8192]{1,0:T(8,128)(2,1)} %param.25, s32[]{:T(128)S(6)} %add.284), kind=kOutput, calls=%fused_computation.40 | convolution fusion | flops 1073741824 | bytes 5242884 | tf_op jit(solution)/shard_map/dot_general | solution.py:468
  157.2 2.9 fusion.22
  161.4 1.3 fusion.26
  165.3 3.2 %add_convert_fusion.3 = bf16[512,1024]{1,0:T(8,128)(2,1)S(1)} fusion(f32[512,1024]{1,0:T(8,128)S(1)} %fusion.32, bf16[1024,4096]{1,0:T(8,128)(2,1)} %collective-permute-done.1, bf16[1024,1024]{1,0:T(8,128)(2,1)} %collective-permute-done), kind=kOutput, calls=%fused_computation.23 | convolution fusion | flops 1074790400 | bytes 6291456 | tf_op jit(solution)/shard_map/dot_general | solution.py:470
  168.5 1.5 collective-permute-start.2
  170.1 3.2 %add_convert_fusion = bf16[512,1024]{1,0:T(8,128)(2,1)S(1)} fusion(f32[512,1024]{1,0:T(8,128)S(1)} %fusion.20, bf16[1024,4096]{1,0:T(8,128)(2,1)} %collective-permute-done.1, bf16[1024,1024]{1,0:T(8,128)(2,1)} %collective-permute-done), kind=kOutput, calls=%fused_computation.17 | convolution fusion | flops 1074790400 | bytes 6291456 | tf_op jit(solution)/shard_map/dot_general | solution.py:470
  173.9 3.2 %add_convert_fusion.1 = bf16[512,1024]{1,0:T(8,128)(2,1)S(1)} fusion(f32[512,1024]{1,0:T(8,128)S(1)} %fusion.24, bf16[1024,4096]{1,0:T(8,128)(2,1)} %collective-permute-done.1, bf16[1024,1024]{1,0:T(8,128)(2,1)} %collective-permute-done), kind=kOutput, calls=%fused_computation.19 | convolution fusion | flops 1074790400 | bytes 6291456 | tf_op jit(solution)/shard_map/dot_general | solution.py:470
  177.0 1.5 collective-permute-start.4
  178.6 3.4 %add_convert_fusion.2 = bf16[512,1024]{1,0:T(8,128)(2,1)S(1)} fusion(f32[512,1024]{1,0:T(8,128)S(1)} %fusion.28, bf16[1024,4096]{1,0:T(8,128)(2,1)} %collective-permute-done.1, bf16[1024,1024]{1,0:T(8,128)(2,1)} %collective-permute-done), kind=kOutput, calls=%fused_computation.21 | convolution fusion | flops 1074790400 | bytes 6291456 | tf_op jit(solution)/shard_map/dot_general | solution.py:470
  182.6 12.0 %collective-permute-done.2 = bf16[512,1024]{1,0:T(8,128)(2,1)S(1)} collective-permute-done((bf16[512,1024]{1,0:T(8,128)(2,1)S(1)}, bf16[512,1024]{1,0:T(8,128)(2,1)S(1)}, u32[]{:S(2)}, u32[]{:S(2)}) %collective-permute-start.2) | collective-permute-done | bytes 1048608 | tf_op jit(solution)/shard_map/ppermute | solution.py:482
  194.6 3.3 %fusion.126 = (f32[512]{0:T(512)S(1)}, f32[512,1024]{1,0:T(8,128)S(1)}) fusion(bf16[512,1024]{1,0:T(8,128)(2,1)S(1)} %collective-permute-done.2, f32[512,1024]{1,0:T(8,128)S(1)} %fusion.34, bf16[1024,4096]{1,0:T(8,128)(2,1)} %collective-permute-done.1, bf16[1024,1024]{1,0:T(8,128)(2,1)} %collective-permute-done), kind=kOutput, calls=%fused_computation.162 | convolution fusion | flops 1075838464 | bytes 8390656 | tf_op jit(solution)/shard_map/dot_general | solution.py:470
  197.9 19.1 %collective-permute-done.5 = bf16[512,1024]{1,0:T(8,128)(2,1)S(1)} collective-permute-done((bf16[512,1024]{1,0:T(8,128)(2,1)S(1)}, bf16[512,1024]{1,0:T(8,128)(2,1)S(1)}, u32[]{:S(2)}, u32[]{:S(2)}) %collective-permute-start.5) | collective-permute-done | bytes 1048608 | tf_op jit(solution)/shard_map/ppermute | solution.py:482
  217.1 3.3 %fusion.125 = (f32[512]{0:T(512)S(1)}, f32[512,1024]{1,0:T(8,128)S(1)}) fusion(bf16[512,1024]{1,0:T(8,128)(2,1)S(1)} %collective-permute-done.5, f32[512,1024]{1,0:T(8,128)S(1)} %fusion.22, bf16[1024,4096]{1,0:T(8,128)(2,1)} %collective-permute-done.1, bf16[1024,1024]{1,0:T(8,128)(2,1)} %collective-permute-done), kind=kOutput, calls=%fused_computation.161 | convolution fusion | flops 1075838464 | bytes 8390656 | tf_op jit(solution)/shard_map/dot_general | solution.py:470
  220.4 19.2 %collective-permute-done.4 = bf16[512,1024]{1,0:T(8,128)(2,1)S(1)} collective-permute-done((bf16[512,1024]{1,0:T(8,128)(2,1)S(1)}, bf16[512,1024]{1,0:T(8,128)(2,1)S(1)}, u32[]{:S(2)}, u32[]{:S(2)}) %collective-permute-start.4) | collective-permute-done | bytes 1048608 | tf_op jit(solution)/shard_map/ppermute | solution.py:482
  239.6 3.3 %fusion.124 = (f32[512]{0:T(512)S(1)}, f32[512,1024]{1,0:T(8,128)S(1)}) fusion(bf16[512,1024]{1,0:T(8,128)(2,1)S(1)} %collective-permute-done.4, f32[512,1024]{1,0:T(8,128)S(1)} %fusion.26, bf16[1024,4096]{1,0:T(8,128)(2,1)} %collective-permute-done.1, bf16[1024,1024]{1,0:T(8,128)(2,1)} %collective-permute-done), kind=kOutput, calls=%fused_computation.160 | convolution fusion | flops 1075838464 | bytes 8390656 | tf_op jit(solution)/shard_map/dot_general | solution.py:470
  242.9 18.6 %collective-permute-done.3 = bf16[512,1024]{1,0:T(8,128)(2,1)S(1)} collective-permute-done((bf16[512,1024]{1,0:T(8,128)(2,1)S(1)}, bf16[512,1024]{1,0:T(8,128)(2,1)S(1)}, u32[]{:S(2)}, u32[]{:S(2)}) %collective-permute-start.3) | collective-permute-done | bytes 1048608 | tf_op jit(solution)/shard_map/ppermute | solution.py:482
  261.5 3.3 %fusion.123 = (f32[512]{0:T(512)S(1)}, f32[512,1024]{1,0:T(8,128)S(1)}) fusion(bf16[512,1024]{1,0:T(8,128)(2,1)S(1)} %collective-permute-done.3, f32[512,1024]{1,0:T(8,128)S(1)} %fusion.30, bf16[1024,4096]{1,0:T(8,128)(2,1)} %collective-permute-done.1, bf16[1024,1024]{1,0:T(8,128)(2,1)} %collective-permute-done), kind=kOutput, calls=%fused_computation.159 | convolution fusion | flops 1075838464 | bytes 8390656 | tf_op jit(solution)/shard_map/dot_general | solution.py:470
  264.9 2.8 exponential_reduce_fusion.2
  268.4 14.2 %stats.1 = f32[4,8,8,512]{3,2,1,0:T(8,128)} custom-call(f32[8,512]{1,0:T(8,128)} %select_maximum_fusion.x_ref), custom_call_target="tpu_custom_call" | custom-call | tf_op jit(solution)/shard_map/stats/pallas_call | solution.py:311
  282.6 1.6 slice_reduce_fusion.2
  285.1 1.3 fusion.112
  286.5 1.9 multiply_add_fusion.1
  (92 shorter events, 18.3 us)
Async XLA Ops:
  0.6 35.6 %copy-start = (bf16[4096,256]{1,0:T(8,128)(2,1)S(1)}, bf16[4096,256]{1,0:T(8,128)(2,1)}, u32[]{:S(2)}) copy-start(bf16[4096,256]{1,0:T(8,128)(2,1)} %param.21) | copy-start | bytes 6291460
  0.7 8.4 %copy-start.7 = (s32[4]{0:T(128)S(1)}, s32[4]{0:T(128)}, u32[]{:S(2)}) copy-start(s32[4]{0:T(128)} %param.16) | copy-start | bytes 52
  0.7 8.5 %copy-start.8 = (s32[4]{0:T(128)S(1)}, s32[4]{0:T(128)}, u32[]{:S(2)}) copy-start(s32[4]{0:T(128)} %param.18) | copy-start | bytes 52
  0.7 8.6 %copy-start.5 = (s32[4,64]{1,0:T(4,128)S(1)}, s32[4,64]{1,0:T(4,128)}, u32[]{:S(2)}) copy-start(s32[4,64]{1,0:T(4,128)} %param.15) | copy-start | bytes 3076
  8.6 27.7 %copy-start.11 = (f32[4096]{0:T(1024)S(1)}, f32[4096]{0:T(1024)}, u32[]{:S(2)}) copy-start(f32[4096]{0:T(1024)} %param.19) | copy-start | bytes 49156
  8.6 156.8 %collective-permute-start.1 = (bf16[1024,4096]{1,0:T(8,128)(2,1)}, bf16[1024,4096]{1,0:T(8,128)(2,1)}, u32[]{:S(2)}, u32[]{:S(2)}) collective-permute-start(bf16[1024,4096]{1,0:T(8,128)(2,1)} %constant_dynamic-slice_fusion), channel_id=1, source_target_pairs={{0,1},{1,0},{2,3},{3,2},{4,5},{5,4},{6,7},{7,6},{8,9},{9,8},{10,11... | collective-permute-start | bytes 25165832 | tf_op jit(solution)/shard_map/ppermute | solution.py:438
  33.9 2.3 copy-start.3
  41.5 1.6 copy-start.4
  46.5 1.8 copy-start.2
  145.7 19.6 %collective-permute-start = (bf16[1024,1024]{1,0:T(8,128)(2,1)}, bf16[1024,1024]{1,0:T(8,128)(2,1)}, u32[]{:S(2)}, u32[]{:S(2)}) collective-permute-start(bf16[1024,1024]{1,0:T(8,128)(2,1)} %bitcast.82), channel_id=1, source_target_pairs={{0,1},{1,0},{2,3},{3,2},{4,5},{5,4},{6,7},{7,6},{8,9},{9,8},{10,11... | collective-permute-start | bytes 6291464 | tf_op jit(solution)/shard_map/ppermute | solution.py:462
  146.1 14.0 %slice-start = ((s8[16777216]{0:T(1024)(128)(4,1)}), s8[4194304]{0:T(1024)(128)(4,1)S(1)}, s32[]{:S(2)}) async-start(s8[16777216]{0:T(1024)(128)(4,1)} %bitcast.83), calls=%async_computation | async-start | bytes 8388608
  148.0 12.1 %slice-start.1 = ((s8[16777216]{0:T(1024)(128)(4,1)}), s8[4194304]{0:T(1024)(128)(4,1)S(1)}, s32[]{:S(2)}) async-start(s8[16777216]{0:T(1024)(128)(4,1)} %bitcast.83), calls=%async_computation.1 | async-start | bytes 8388608
  151.0 9.1 %slice-start.2 = ((s8[16777216]{0:T(1024)(128)(4,1)}), s8[4194304]{0:T(1024)(128)(4,1)S(1)}, s32[]{:S(2)}) async-start(s8[16777216]{0:T(1024)(128)(4,1)} %bitcast.83), calls=%async_computation.2 | async-start | bytes 8388608
  154.2 5.9 %slice-start.3 = ((s8[16777216]{0:T(1024)(128)(4,1)}), s8[4194304]{0:T(1024)(128)(4,1)S(1)}, s32[]{:S(2)}) async-start(s8[16777216]{0:T(1024)(128)(4,1)} %bitcast.83), calls=%async_computation.3 | async-start | bytes 8388608
  168.5 26.1 %collective-permute-start.2 = (bf16[512,1024]{1,0:T(8,128)(2,1)S(1)}, bf16[512,1024]{1,0:T(8,128)(2,1)S(1)}, u32[]{:S(2)}, u32[]{:S(2)}) collective-permute-start(bf16[512,1024]{1,0:T(8,128)(2,1)S(1)} %add_convert_fusion.3), channel_id=1, source_target_pairs={{0,2},{1,3},{2,0},{3,1},{4,6},{5,7},{6,4},{7,5},{8,10},{9,11},{10,... | collective-permute-start | bytes 3145736 | tf_op jit(solution)/shard_map/ppermute | solution.py:482
  173.2 43.8 %collective-permute-start.5 = (bf16[512,1024]{1,0:T(8,128)(2,1)S(1)}, bf16[512,1024]{1,0:T(8,128)(2,1)S(1)}, u32[]{:S(2)}, u32[]{:S(2)}) collective-permute-start(bf16[512,1024]{1,0:T(8,128)(2,1)S(1)} %add_convert_fusion), channel_id=1, source_target_pairs={{0,2},{1,3},{2,0},{3,1},{4,6},{5,7},{6,4},{7,5},{8,10},{9,11},{10,... | collective-permute-start | bytes 3145736 | tf_op jit(solution)/shard_map/ppermute | solution.py:482
  177.0 62.5 %collective-permute-start.4 = (bf16[512,1024]{1,0:T(8,128)(2,1)S(1)}, bf16[512,1024]{1,0:T(8,128)(2,1)S(1)}, u32[]{:S(2)}, u32[]{:S(2)}) collective-permute-start(bf16[512,1024]{1,0:T(8,128)(2,1)S(1)} %add_convert_fusion.1), channel_id=1, source_target_pairs={{0,2},{1,3},{2,0},{3,1},{4,6},{5,7},{6,4},{7,5},{8,10},{9,11},{10,... | collective-permute-start | bytes 3145736 | tf_op jit(solution)/shard_map/ppermute | solution.py:482
  182.0 79.5 %collective-permute-start.3 = (bf16[512,1024]{1,0:T(8,128)(2,1)S(1)}, bf16[512,1024]{1,0:T(8,128)(2,1)S(1)}, u32[]{:S(2)}, u32[]{:S(2)}) collective-permute-start(bf16[512,1024]{1,0:T(8,128)(2,1)S(1)} %add_convert_fusion.2), channel_id=1, source_target_pairs={{0,2},{1,3},{2,0},{3,1},{4,6},{5,7},{6,4},{7,5},{8,10},{9,11},{10,... | collective-permute-start | bytes 3145736 | tf_op jit(solution)/shard_map/ppermute | solution.py:482
  264.9 19.7 %copy-start.9 = (f32[22]{0:T(128)S(1)}, f32[22]{0:T(128)}, u32[]{:S(2)}) copy-start(f32[22]{0:T(128)} %param.26) | copy-start | bytes 268
  264.9 19.7 %copy-start.10 = (f32[22]{0:T(128)S(1)}, f32[22]{0:T(128)}, u32[]{:S(2)}) copy-start(f32[22]{0:T(128)} %param.27) | copy-start | bytes 268
  264.9 24.0 %copy-start.1 = (bf16[4096,256]{1,0:T(8,128)(2,1)S(1)}, bf16[4096,256]{1,0:T(8,128)(2,1)}, u32[]{:S(2)}) copy-start(bf16[4096,256]{1,0:T(8,128)(2,1)} %param.21) | copy-start | bytes 6291460
  285.1 3.8 %copy-start.6 = (f32[22]{0:T(128)}, f32[22]{0:T(128)S(1)}, u32[]{:S(2)}) copy-start(f32[22]{0:T(128)S(1)} %get-tuple-element.20) | copy-start | bytes 268
